TPU v7x, 32 devices: a whole 2x2x4 slice. The times are simulated.
32 devices in a mesh: seq: 8 (over z, x), mp: 4 (over y, core).
Axes of the slice: x: 2, y: 2, z: 4, core: 2. Of those that a mesh axis runs over, the one named last changes fastest.
Arguments:
- tokens: bfloat16 [32768, 1152], P(('seq', 'mp')), may hold values from -6 to 6
- cotangent: bfloat16 [32768, 1152], P(('seq', 'mp')), may hold values from -6 to 6
- segment: int32 [32768], P(('seq', 'mp')), may hold values from 0 to 3, as said below
- timestep: int32 [128], P(('seq', 'mp')), may hold values from 0 to 999
- head_mask: int32 [128, 16], P(('seq', 'mp')), may hold values 0 or 1
- chan_mask: int32 [128, 16], P(('seq', 'mp')), may hold values 0 or 1
- router_keep: int32 [32768], P(('seq', 'mp')), may hold values from 0 to 1, as said below
- ada_weight: bfloat16 [1152, 6912], P('mp'), may hold values from -0.1875 to 0.1875
- ada_bias: bfloat16 [6912], replicated, may hold values from -3 to 3
- qkv_weight: bfloat16 [1152, 3456], P('mp'), may hold values from -0.1875 to 0.1875
- qv_bias: bfloat16 [2304], replicated, may hold values from -2 to 2
- proj_weight: bfloat16 [1152, 1152], P('mp'), may hold values from -0.5 to 0.5
- proj_bias: bfloat16 [1152], replicated, may hold values from -2 to 2
- up_weight: bfloat16 [1152, 4608], P('mp'), may hold values from -0.1875 to 0.1875
- up_bias: bfloat16 [4608], replicated, may hold values from -2 to 2
- down_weight: bfloat16 [4608, 1152], P('mp'), may hold values from -0.09375 to 0.09375
- down_bias: bfloat16 [1152], replicated, may hold values from -2 to 2
Outputs:
- output: bfloat16 [32768, 1152], P(('seq', 'mp'))
- token_grad: float32 [32768, 1152], P(('seq', 'mp'))
- ada_weight_grad: float32 [1152, 6912], P('mp', 'seq')
- qkv_weight_grad: float32 [1152, 3456], P('mp', 'seq')
- proj_weight_grad: float32 [1152, 1152], P('mp', 'seq')
- up_weight_grad: float32 [1152, 4608], P('mp', 'seq')
- down_weight_grad: float32 [4608, 1152], P('mp', 'seq')
- ada_bias_grad: float32 [6912], replicated
- qv_bias_grad: float32 [2304], replicated
- proj_bias_grad: float32 [1152], replicated
- up_bias_grad: float32 [4608], replicated
- down_bias_grad: float32 [1152], replicated
Inputs may be any that keep to these rules, and one draw needn't show every extreme that they name: The 1024 tokens of each device are one item (segment 0 throughout) or 4 items of 256 tokens with segments 0 to 3 in order; exactly half of the devices hold one item, and their unused item slots do not matter. `router_keep`: exactly 24576 entries are 1; how many of a device's tokens are kept differs from device to device.
All inputs are finite; a program needn't handle non-finite values. No bound on the sum of `head_mask` or of `chan_mask` on one device may be relied on, other than what follows from the above.
Results may differ from a plain program's by a relative error of at most 0.012.
Values may be sent and summed in bfloat16 or wider, within the bound.
No kernel may reach another device: no remote copies, remote signals or barrier semaphores. Data moves between devices by JAX's collectives and lax.ppermute only.
A program may use at most 320 MiB of HBM per device.

v0:
```python
from functools import partial
import math

import jax
import jax.numpy as jnp
from jax import lax
from jax.sharding import PartitionSpec as P

KEEP_DEV = 768


HIGHEST = lax.Precision.HIGHEST


def sinusoid(stamps, model_width):
    half_width = model_width // 2
    frequency = jnp.exp(
        -math.log(10000.0) * jnp.arange(half_width).astype(jnp.float32) / half_width
    )
    angles = stamps.astype(jnp.float32)[:, None] * frequency[None, :]
    return jnp.concatenate([jnp.cos(angles), jnp.sin(angles)], axis=1)


def normalize(values):
    center = values - jnp.mean(values, axis=1, keepdims=True)
    return center * lax.rsqrt(jnp.mean(center * center, axis=1, keepdims=True) + 1e-06)


def modulate(values, scale_rows, shift_rows):
    return normalize(values) * (1.0 + scale_rows) + shift_rows


def split_heads(values, head_count):
    row_count, model_width = values.shape
    return values.reshape(row_count, head_count, model_width // head_count).transpose(1, 0, 2)


def merge_heads(values):
    head_count, row_count, head_size = values.shape
    return values.transpose(1, 0, 2).reshape(row_count, head_count * head_size)


def masked_scores(head_queries, head_keys, same_item, score_scale):
    scores = (
        jnp.einsum("qe,ke->qk", head_queries, head_keys, preferred_element_type=jnp.float32)
        * score_scale
    )
    return jnp.where(same_item, scores, -1e30)


def attend_forward(triple, same_item, score_scale):
    head_queries, head_keys, head_values = triple
    scores = masked_scores(head_queries, head_keys, same_item, score_scale)
    row_max = jnp.max(scores, axis=1, keepdims=True)
    exp_scores = jnp.exp(scores - row_max)
    row_total = jnp.sum(exp_scores, axis=1, keepdims=True)
    attention = (exp_scores / row_total).astype(jnp.bfloat16)
    result = jnp.dot(attention, head_values, preferred_element_type=jnp.float32)
    return (result, (row_max + jnp.log(row_total))[:, 0])


def attend_backward(quintet, same_item, score_scale):
    head_queries, head_keys, head_values, head_grad, log_total = quintet
    scores = masked_scores(head_queries, head_keys, same_item, score_scale)
    probs_full = jnp.exp(scores - log_total[:, None])
    attention = probs_full.astype(jnp.bfloat16)
    grad_soft = jnp.einsum("qe,ke->qk", head_grad, head_values, preferred_element_type=jnp.float32)
    row_inner = jnp.sum(grad_soft * probs_full, axis=1, keepdims=True)
    grad_scores = (probs_full * (grad_soft - row_inner)).astype(jnp.bfloat16)
    grad_queries = jnp.dot(grad_scores, head_keys, preferred_element_type=jnp.float32) * score_scale
    grad_keys = (
        jnp.einsum("qk,qe->ke", grad_scores, head_queries, preferred_element_type=jnp.float32)
        * score_scale
    )
    grad_values = jnp.einsum("qk,qe->ke", attention, head_grad, preferred_element_type=jnp.float32)
    return (grad_queries, grad_keys, grad_values)


def feed_forward(rows_in, gate_rows, up_weight, up_bias, down_weight, down_bias):
    pre_act = jnp.dot(rows_in, up_weight, preferred_element_type=jnp.float32) + up_bias.astype(
        jnp.float32
    )
    row_count, hidden_width = pre_act.shape
    group_count = gate_rows.shape[1]
    activated = jax.nn.gelu(pre_act, approximate=True).reshape(
        row_count, group_count, hidden_width // group_count
    )
    activated = activated * gate_rows.astype(jnp.float32)[:, :, None]
    hidden = activated.reshape(row_count, hidden_width).astype(jnp.bfloat16)
    mlp_out = (
        jnp.dot(hidden, down_weight, preferred_element_type=jnp.float32)
        + down_bias.astype(jnp.float32)
    ).astype(jnp.bfloat16)
    return (pre_act, hidden, mlp_out)


def feed_backward(rows_in, gate_rows, pre_act, hidden, grad_out, up_weight, down_weight):
    row_count, hidden_width = pre_act.shape
    group_count = gate_rows.shape[1]
    grad_hidden = jnp.einsum("nd,fd->nf", grad_out, down_weight, preferred_element_type=jnp.float32)
    grad_hidden = (
        grad_hidden.reshape(row_count, group_count, hidden_width // group_count)
        * gate_rows.astype(jnp.float32)[:, :, None]
    )
    grad_hidden = grad_hidden.reshape(row_count, hidden_width)
    gelu_value, gelu_back = jax.vjp(partial(jax.nn.gelu, approximate=True), pre_act)
    grad_pre = gelu_back(grad_hidden)[0].astype(jnp.bfloat16)
    down_grad = jnp.einsum("nf,nd->fd", hidden, grad_out, preferred_element_type=jnp.float32)
    up_grad = jnp.einsum("nd,nf->df", rows_in, grad_pre, preferred_element_type=jnp.float32)
    grad_rows = jnp.einsum(
        "nf,df->nd", grad_pre, up_weight, preferred_element_type=jnp.float32
    ).astype(jnp.bfloat16)
    up_bias_grad = jnp.sum(grad_pre.astype(jnp.float32), axis=0)
    down_bias_grad = jnp.sum(grad_out.astype(jnp.float32), axis=0)
    return (grad_rows, up_grad, up_bias_grad, down_grad, down_bias_grad)


def on_device(
    tokens,
    cotangent,
    segment,
    timestep,
    head_mask,
    chan_mask,
    router_keep,
    ada_weight,
    ada_bias,
    qkv_weight,
    qv_bias,
    proj_weight,
    proj_bias,
    up_weight,
    up_bias,
    down_weight,
    down_bias,
):
    row_count, model_width = tokens.shape
    slot_count = timestep.shape[0]
    head_count = head_mask.shape[1]
    score_scale = (model_width // head_count) ** (-0.5)
    gathered = (
        lax.all_gather(ada_weight, "mp", axis=0, tiled=True),
        lax.all_gather(qkv_weight, "mp", axis=0, tiled=True),
        lax.all_gather(proj_weight, "mp", axis=0, tiled=True),
        lax.all_gather(up_weight, "mp", axis=0, tiled=True),
        lax.all_gather(down_weight, "mp", axis=0, tiled=True),
    )
    full_ada, full_qkv, full_proj, full_up, full_down = gathered
    condition = jax.nn.silu(sinusoid(timestep, model_width)).astype(jnp.bfloat16)
    modulation = jnp.dot(condition, full_ada, preferred_element_type=jnp.float32) + ada_bias.astype(
        jnp.float32
    )
    one_hot = (segment[:, None] == jnp.arange(slot_count)[None, :]).astype(jnp.float32)
    tok_mod = jnp.dot(one_hot, modulation, precision=HIGHEST)
    first_shift, first_scale, first_gate, second_shift, second_scale, second_gate = [
        tok_mod[:, section * model_width : (section + 1) * model_width] for section in range(6)
    ]
    head_gate = jnp.dot(one_hot, head_mask.astype(jnp.float32), precision=HIGHEST)
    chan_gate = jnp.dot(one_hot, chan_mask.astype(jnp.float32), precision=HIGHEST).astype(
        jnp.bfloat16
    )
    keep_rows = router_keep.astype(jnp.float32)[:, None]
    tok_float = tokens.astype(jnp.float32)
    normed_val, first_back = jax.vjp(modulate, tok_float, first_scale, first_shift)
    normed = normed_val.astype(jnp.bfloat16)
    joined = jnp.dot(normed, full_qkv, preferred_element_type=jnp.float32)
    qv_float = qv_bias.astype(jnp.float32)
    queries = (joined[:, :model_width] + qv_float[:model_width]).astype(jnp.bfloat16)
    keys_all = joined[:, model_width : 2 * model_width].astype(jnp.bfloat16)
    values_all = (joined[:, 2 * model_width :] + qv_float[model_width:]).astype(jnp.bfloat16)
    same_item = segment[:, None] == segment[None, :]
    head_inputs = (
        split_heads(queries, head_count),
        split_heads(keys_all, head_count),
        split_heads(values_all, head_count),
    )
    attended, log_total = lax.map(
        lambda triple: attend_forward(triple, same_item, score_scale), head_inputs
    )
    attn_cat = merge_heads(attended * head_gate.T[:, :, None]).astype(jnp.bfloat16)
    branch = jnp.dot(attn_cat, full_proj, preferred_element_type=jnp.float32) + proj_bias.astype(
        jnp.float32
    )
    middle = tok_float + first_gate * branch
    second_val, second_back = jax.vjp(modulate, middle, second_scale, second_shift)
    second_in = second_val.astype(jnp.bfloat16)
    device_count = lax.axis_size(("seq", "mp"))
    device_index = lax.axis_index(("seq", "mp"))
    slot_rows = -(-row_count // device_count)
    buffer_rows = device_count * slot_rows
    kept_here = jnp.sum(router_keep).reshape(1)
    counts = lax.all_gather(kept_here, ("seq", "mp"), axis=0, tiled=True)
    kept_before = jnp.cumsum(counts) - counts
    local_rank = jnp.cumsum(router_keep) - router_keep
    global_rank = kept_before[device_index] + local_rank
    send_slot = jnp.where(
        router_keep == 1,
        global_rank % device_count * slot_rows + local_rank // device_count,
        buffer_rows,
    )
    source_rank = ((device_index - kept_before) % device_count)[:, None] + jnp.arange(slot_rows)[
        None, :
    ] * device_count
    arrived = (source_rank < counts[:, None]).reshape(buffer_rows)
    dest_row = jnp.where(
        arrived,
        ((kept_before[:, None] + source_rank) // device_count).reshape(buffer_rows),
        KEEP_DEV,
    )

    def to_owner(values):
        placed = (
            jnp.zeros((buffer_rows,) + values.shape[1:], values.dtype)
            .at[send_slot]
            .set(values, mode="drop")
        )
        return placed.reshape((device_count, slot_rows) + values.shape[1:])

    def compact(values):
        flat_rows = values.reshape((buffer_rows,) + values.shape[2:])
        return (
            jnp.zeros((KEEP_DEV,) + flat_rows.shape[1:], flat_rows.dtype)
            .at[dest_row]
            .set(flat_rows, mode="drop")
        )

    def spread(values):
        picked = jnp.take(values, jnp.minimum(dest_row, KEEP_DEV - 1), axis=0)
        picked = jnp.where(arrived[:, None], picked, jnp.zeros_like(picked))
        return picked.reshape((device_count, slot_rows) + values.shape[1:])

    def to_source(values):
        flat_rows = values.reshape((buffer_rows,) + values.shape[2:])
        picked = jnp.take(flat_rows, jnp.minimum(send_slot, buffer_rows - 1), axis=0)
        return jnp.where(router_keep[:, None] == 1, picked, jnp.zeros_like(picked))

    sent_rows, sent_gate = (
        lax.all_to_all(to_owner(second_in), ("seq", "mp"), split_axis=0, concat_axis=0, tiled=True),
        lax.all_to_all(to_owner(chan_gate), ("seq", "mp"), split_axis=0, concat_axis=0, tiled=True),
    )
    owner_rows = compact(sent_rows)
    owner_gate = compact(sent_gate)
    pre_act, hidden, owner_out = feed_forward(
        owner_rows, owner_gate, full_up, up_bias, full_down, down_bias
    )
    mlp_out = to_source(
        lax.all_to_all(spread(owner_out), ("seq", "mp"), split_axis=0, concat_axis=0, tiled=True)
    )
    mlp_float = mlp_out.astype(jnp.float32)
    output = (middle + keep_rows * second_gate * mlp_float).astype(jnp.bfloat16)
    grad_final = cotangent.astype(jnp.float32)
    grad_out = (keep_rows * second_gate * grad_final).astype(jnp.bfloat16)
    grad_second_gate = keep_rows * grad_final * mlp_float
    owner_grad = compact(
        lax.all_to_all(to_owner(grad_out), ("seq", "mp"), split_axis=0, concat_axis=0, tiled=True)
    )
    owner_back, up_grad, up_bias_grad, down_grad, down_bias_grad = feed_backward(
        owner_rows, owner_gate, pre_act, hidden, owner_grad, full_up, full_down
    )
    grad_second = to_source(
        lax.all_to_all(spread(owner_back), ("seq", "mp"), split_axis=0, concat_axis=0, tiled=True)
    )
    grad_middle_part, grad_second_scale, grad_second_shift = second_back(
        grad_second.astype(jnp.float32)
    )
    grad_middle = grad_final + grad_middle_part
    grad_branch = (first_gate * grad_middle).astype(jnp.bfloat16)
    grad_first_gate = grad_middle * branch
    proj_grad = jnp.einsum("nd,ne->de", attn_cat, grad_branch, preferred_element_type=jnp.float32)
    proj_bias_grad = jnp.sum(grad_branch.astype(jnp.float32), axis=0)
    grad_cat = jnp.einsum(
        "ne,de->nd", grad_branch, full_proj, preferred_element_type=jnp.float32
    ).astype(jnp.bfloat16)
    grad_heads = split_heads(grad_cat, head_count) * head_gate.T[:, :, None].astype(jnp.bfloat16)
    grad_queries, grad_keys, grad_values = lax.map(
        lambda quintet: attend_backward(quintet, same_item, score_scale),
        head_inputs + (grad_heads, log_total),
    )
    grad_joined = jnp.concatenate(
        [merge_heads(grad_queries), merge_heads(grad_keys), merge_heads(grad_values)], axis=1
    ).astype(jnp.bfloat16)
    qkv_grad = jnp.einsum("nd,ne->de", normed, grad_joined, preferred_element_type=jnp.float32)
    column_sums = jnp.sum(grad_joined.astype(jnp.float32), axis=0)
    qv_bias_grad = jnp.concatenate([column_sums[:model_width], column_sums[2 * model_width :]])
    grad_normed = jnp.einsum("ne,de->nd", grad_joined, full_qkv, preferred_element_type=jnp.float32)
    grad_tok_part, grad_first_scale, grad_first_shift = first_back(grad_normed)
    token_grad = grad_middle + grad_tok_part
    grad_tok_mod = jnp.concatenate(
        [
            grad_first_shift,
            grad_first_scale,
            grad_first_gate,
            grad_second_shift,
            grad_second_scale,
            grad_second_gate,
        ],
        axis=1,
    )
    grad_modulation = jnp.einsum("ns,nc->sc", one_hot, grad_tok_mod, precision=HIGHEST)
    ada_bias_grad = jnp.sum(grad_modulation, axis=0)
    weight_grads = (qkv_grad, proj_grad, up_grad, down_grad)
    partial_sums = (
        lax.psum_scatter(weight_grads[0], "seq", scatter_dimension=1, tiled=True),
        lax.psum_scatter(weight_grads[1], "seq", scatter_dimension=1, tiled=True),
        lax.psum_scatter(weight_grads[2], "seq", scatter_dimension=1, tiled=True),
        lax.psum_scatter(weight_grads[3], "seq", scatter_dimension=1, tiled=True),
    )
    reduced = (
        lax.psum_scatter(partial_sums[0], "mp", scatter_dimension=0, tiled=True),
        lax.psum_scatter(partial_sums[1], "mp", scatter_dimension=0, tiled=True),
        lax.psum_scatter(partial_sums[2], "mp", scatter_dimension=0, tiled=True),
        lax.psum_scatter(partial_sums[3], "mp", scatter_dimension=0, tiled=True),
    )
    reduced = tuple(reduced)
    all_condition, all_modulation = (
        lax.all_gather(condition.astype(jnp.float32), ("seq", "mp"), axis=0, tiled=True),
        lax.all_gather(grad_modulation, ("seq", "mp"), axis=0, tiled=True),
    )
    row_width = model_width // lax.axis_size("mp")
    col_width = 6 * model_width // lax.axis_size("seq")
    cond_cols = lax.dynamic_slice_in_dim(
        all_condition, lax.axis_index("mp") * row_width, row_width, 1
    )
    mod_cols = lax.dynamic_slice_in_dim(
        all_modulation, lax.axis_index("seq") * col_width, col_width, 1
    )
    ada_piece = jnp.einsum("sd,sc->dc", cond_cols, mod_cols, precision=HIGHEST)
    reduced = (ada_piece,) + reduced
    bias_grads = lax.psum(
        (ada_bias_grad, qv_bias_grad, proj_bias_grad, up_bias_grad, down_bias_grad), ("seq", "mp")
    )
    return (output, token_grad) + reduced + tuple(bias_grads)


def solution(mesh):
    in_specs = (
        P(("seq", "mp"), None),
        P(("seq", "mp"), None),
        P(("seq", "mp")),
        P(("seq", "mp")),
        P(("seq", "mp"), None),
        P(("seq", "mp"), None),
        P(("seq", "mp")),
        P("mp", None),
        P(),
        P("mp", None),
        P(),
        P("mp", None),
        P(),
        P("mp", None),
        P(),
        P("mp", None),
        P(),
    )
    out_specs = (
        P(("seq", "mp"), None),
        P(("seq", "mp"), None),
        P("mp", "seq"),
        P("mp", "seq"),
        P("mp", "seq"),
        P("mp", "seq"),
        P("mp", "seq"),
        P(),
        P(),
        P(),
        P(),
        P(),
    )
    return jax.shard_map(
        on_device, mesh=mesh, in_specs=in_specs, out_specs=out_specs, check_vma=False
    )
```

profile of v0, /device:TPU:0, one launch (start us, length us, event | category | flops | bytes accessed | tf_op | source)
XLA Modules:
  0.0 2140.3 jit_solution(18268267810001325600)
XLA Ops:
  11.4 42.8 %all-reduce = s32[32]{0:T(128)S(1)} all-reduce(s32[32]{0:T(128)S(1)} %dynamic-update-slice), channel_id=1, replica_groups=mesh['seq'=8,'mp'=4] {'seq','mp'}, use_global_device_ids=true, to_apply=%add | all-reduce | flops 32 | bytes 256
  70.2 44.4 %all-gather.9.cloned.1.call-done = bf16[1152,6912]{1,0:T(8,128)(2,1)} async-done(((bf16[288,6912]{1,0:T(8,128)(2,1)}), bf16[1152,6912]{1,0:T(8,128)(2,1)}) %all-gather.9.cloned.1.call-update) | async-done | bytes 15925264 | tf_op jit(solution)/shard_map/all_gather | solution.py:142
  146.4 25.6 %all-gather.11.cloned.1.call-done = bf16[1152,3456]{1,0:T(8,128)(2,1)} async-done(((bf16[288,3456]{1,0:T(8,128)(2,1)}), bf16[1152,3456]{1,0:T(8,128)(2,1)}) %all-gather.11.cloned.1.call-update) | async-done | bytes 7962640 | tf_op jit(solution)/shard_map/all_gather | solution.py:143
  234.4 171.1 %while.30 = (s32[]{:T(128)}, f32[16,1024,72]{1,2,0:T(8,128)}, f32[16,1024]{1,0:T(8,128)}, bf16[16,1024,72]{2,1,0:T(8,128)(2,1)}, bf16[16,1024,72]{2,1,0:T(8,128)...) while((s32[]{:T(128)}, f32[16,1024,72]{1,2,0:T(8,128)}, ...), condition=%wide.region_5.6_spmd.clone.clone, body=%wide.region_2.5_spmd.clone.sunk.clone | while | flops 317717504 | bytes 30505076 | solution.py:177
  451.9 15.2 copy.145
  473.7 20.6 all-to-all-done
  501.0 21.7 %multiply_convert_fusion.1 = (bf16[768,4608]{1,0:T(8,128)(2,1)}, f32[768,4608]{1,0:T(8,128)}) fusion(f32[768,4608]{1,0:T(8,128)} %copy.145, f32[4608]{0:T(1024)} %convert_element_type.148, bf16[768,1152]{1,0:T(8,128)(2,1)S(1)} %scatter_custom_fusion.1, bf16[1152,4608]{1,0:T(8,128)(2,1)} %all-gather.15.cloned.1.call-done), kind=kOutput, calls=%fused_computation.77 | convolution fusion | flops 8192655360 | bytes 47794176 | tf_op jit(solution)/shard_map/dot_general | solution.py:80
  522.7 22.2 %convert_reduce_fusion = (f32[4608]{0:T(1024)}, bf16[768,4608]{1,0:T(8,128)(2,1)S(1)}) fusion(f32[768,4608]{1,0:T(8,128)} %get-tuple-element.417, f32[4608]{0:T(1024)} %convert_element_type.148, f32[768,4608]{1,0:T(8,128)} %copy.145, bf16[768,1152]{1,0:T(8,128)(2,1)S(1)} %scatter_custom_fusion.5, bf16[4608,1152]{1,0:T(8,128)(2,1)} %all-gather.17.cloned.1.call-done), kind=kOutput, calls=%fused_computation.75 | convolution fusion | flops 8238657024 | bytes 47812608 | tf_op jit(solution)/shard_map/nd,fd->nf/dot_general | solution.py:100
  588.5 59.9 %all_to_all.25 = bf16[32,32,1152]{2,1,0:T(8,128)(2,1)} all-to-all(bf16[32,32,1152]{2,1,0:T(8,128)(2,1)S(1)} %bitcast.215), channel_id=1, replica_groups=mesh['seq'=8,'mp'=4] {'seq','mp'}, dimensions={0} | all-to-all | bytes 4718592 | tf_op jit(solution)/shard_map/all_to_all | solution.py:247
  663.4 42.1 %all-to-all-done.4 = bf16[32,32,1152]{2,1,0:T(8,128)(2,1)S(1)} async-done(((bf16[32,32,1152]{2,1,0:T(8,128)(2,1)}), bf16[32,32,1152]{2,1,0:T(8,128)(2,1)S(1)}, u32[]{:S(2)}, u32[]{:S(2)}) %all-to-all-start.4) | async-done | bytes 2359328 | tf_op jit(solution)/shard_map/all_to_all | solution.py:261
  751.5 192.2 %while.31 = (s32[]{:T(128)}, bf16[16,1024,72]{1,2,0:T(8,128)(2,1)S(1)}, bf16[16,1024,72]{1,2,0:T(8,128)(2,1)}, bf16[16,1024,72]{1,2,0:T(8,128)(2,1)}, bf16[16,10...) while((s32[]{:T(128)}, ...), condition=%wide.region_22.25_spmd.clone.clone, body=%wide.region_20.24_spmd.clone.sunk.clone | while | flops 765606912 | bytes 33981552 | solution.py:275
  943.7 18.0 fusion.127
  963.3 15.0 fusion.142
  979.7 15.7 fusion.141
  995.5 17.1 constant_dynamic-update-slice_fusion
  1037.5 14.8 fusion.138
  1055.0 175.0 %reduce-scatter.15.cloned.1.call-done = f32[1152,432]{0,1:T(8,128)} async-done(((f32[1152,3456]{0,1:T(8,128)}), f32[1152,432]{0,1:T(8,128)}) %reduce-scatter.15.cloned.1.call-update) | async-done | bytes 1990672 | tf_op jit(solution)/shard_map/reduce_scatter | solution.py:303
  1233.2 346.5 %reduce-scatter.21.cloned.1.call-done = f32[4608,144]{0,1:T(8,128)} async-done(((f32[4608,1152]{0,1:T(8,128)}), f32[4608,144]{0,1:T(8,128)}) %reduce-scatter.21.cloned.1.call-update) | async-done | bytes 2654224 | tf_op jit(solution)/shard_map/reduce_scatter | solution.py:306
  1579.8 349.6 %reduce-scatter.19.cloned.1.call-done = f32[1152,576]{0,1:T(8,128)} async-done(((f32[1152,4608]{0,1:T(8,128)}), f32[1152,576]{0,1:T(8,128)}) %reduce-scatter.19.cloned.1.call-update) | async-done | bytes 2654224 | tf_op jit(solution)/shard_map/reduce_scatter | solution.py:305
  1933.0 41.6 %all-gather = f32[32,4,1152]{2,1,0:T(4,128)S(1)} all-gather(f32[1,4,1152]{2,1,0:T(4,128)S(1)} %bitcast_convert_fusion), channel_id=1, replica_groups=mesh['seq'=8,'mp'=4] {'seq','mp'}, dimensions={0}, use_global_device_ids=true | all-gather | bytes 608256 | tf_op jit(solution)/shard_map/all_gather | solution.py:316
  1981.8 39.3 %all-reduce.1 = (f32[6912]{0:T(1024)}, f32[2304]{0:T(1024)}, f32[1152]{0:T(1024)}, f32[4608]{0:T(1024)}, f32[1152]{0:T(1024)}) all-reduce(f32[6912]{0:T(1024)S(1)} %get-tuple-element.422, f32[2304]{0:T(1024)S(1)} %pad_maximum_fusion.2, f32[1152]{0:T(1024)S(1)} %copy-done.52, ...), channel_id=1, replica_groups=mesh['seq'=8,'mp'=4] {'seq','mp'}, use_global_device_ids=true, to_apply=%region_34.37 | all-reduce | flops 16128 | bytes 129024 | tf_op jit(solution)/shard_map/psum | solution.py:329
  2029.6 26.4 %reduce-scatter.25.cloned.1.call-done = f32[288,432]{1,0:T(8,128)} async-done(((f32[1152,432]{1,0:T(8,128)}), f32[288,432]{1,0:T(8,128)}) %reduce-scatter.25.cloned.1.call-update) | async-done | bytes 497680
  2055.9 37.7 %reduce-scatter.23.cloned.1.call-done = f32[1152,144]{0,1:T(8,128)} async-done(((f32[4608,144]{0,1:T(8,128)}), f32[1152,144]{0,1:T(8,128)}) %reduce-scatter.23.cloned.1.call-update) | async-done | bytes 663568 | tf_op jit(solution)/shard_map/reduce_scatter | solution.py:312
  2093.7 39.6 %reduce-scatter.29.cloned.1.call-done = f32[288,576]{1,0:T(8,128)} async-done(((f32[1152,576]{1,0:T(8,128)}), f32[288,576]{1,0:T(8,128)}) %reduce-scatter.29.cloned.1.call-update) | async-done | bytes 663568
  (518 shorter events, 692.7 us)
Async XLA Ops:
  7.2 107.4 %all-gather.9.cloned.1.call-start = ((), (), s32[]{:S(2)}) async-start(), calls=%async_computation.13 | async-start | bytes 19906560 | tf_op jit(solution)/shard_map/all_gather | solution.py:142
  7.9 164.1 %all-gather.11.cloned.1.call-start = ((), (), s32[]{:S(2)}) async-start(), calls=%async_computation.14 | async-start | bytes 9953280 | tf_op jit(solution)/shard_map/all_gather | solution.py:143
  8.7 401.2 %all-gather.13.cloned.1.call-start = ((), (), s32[]{:S(2)}) async-start(), calls=%async_computation.15 | async-start | bytes 3317760 | tf_op jit(solution)/shard_map/all_gather | solution.py:144
  9.5 491.6 %all-gather.15.cloned.1.call-start = ((), (), s32[]{:S(2)}) async-start(), calls=%async_computation.16 | async-start | bytes 13271040 | tf_op jit(solution)/shard_map/all_gather | solution.py:145
  10.7 209.5 %copy-start.32 = (f32[1024]{0:T(1024)}, f32[1024]{0:T(1024)S(1)}, u32[]{:S(2)}) copy-start(f32[1024]{0:T(1024)S(1)} %get-tuple-element.412) | copy-start | bytes 12292
  62.4 166.9 %all-to-all-start.1 = ((bf16[32,2,256]{2,1,0:T(2,128)(2,1)}), bf16[32,2,256]{2,1,0:T(2,128)(2,1)S(1)}, u32[]{:S(2)}, u32[]{:S(2)}) async-start(bf16[32,2,256]{2,1,0:T(2,128)(2,1)} %reshape.511), calls=%async_computation.1 | async-start | bytes 65536 | tf_op jit(solution)/shard_map/all_to_all | solution.py:239
  67.0 455.7 %all-gather.17.cloned.1.call-start = ((), (), s32[]{:S(2)}) async-start(), calls=%async_computation.17 | async-start | bytes 13271040 | tf_op jit(solution)/shard_map/all_gather | solution.py:146
  68.0 66.4 %copy-start.26 = (f32[1024]{0:T(1024)}, f32[1024]{0:T(1024)S(1)}, u32[]{:S(2)}) copy-start(f32[1024]{0:T(1024)S(1)} %broadcast_multiply_fusion.2) | copy-start | bytes 12292
  229.2 204.2 %all-to-all-start.3 = ((bf16[32,32,1152]{2,1,0:T(8,128)(2,1)}), bf16[32,32,1152]{2,1,0:T(8,128)(2,1)}, u32[]{:S(2)}, u32[]{:S(2)}) async-start(bf16[32,32,1152]{2,1,0:T(8,128)(2,1)} %bitcast.220), calls=%async_computation.3 | async-start | bytes 4718592 | tf_op jit(solution)/shard_map/all_to_all | solution.py:255
  420.4 296.8 %copy-start.24 = (f32[1024]{0:T(1024)}, f32[1024]{0:T(1024)S(1)}, u32[]{:S(2)}) copy-start(f32[1024]{0:T(1024)S(1)} %broadcast_multiply_fusion.1) | copy-start | bytes 12292
  423.1 294.0 %copy-start.37 = (f32[1024]{0:T(1024)}, f32[1024]{0:T(1024)S(1)}, u32[]{:S(2)}) copy-start(f32[1024]{0:T(1024)S(1)} %fusion.120) | copy-start | bytes 12292
  433.4 60.8 %all-to-all-start = ((bf16[32,32,1152]{2,1,0:T(8,128)(2,1)}), bf16[32,32,1152]{2,1,0:T(8,128)(2,1)}, u32[]{:S(2)}, u32[]{:S(2)}) async-start(bf16[32,32,1152]{2,1,0:T(8,128)(2,1)} %bitcast.15), calls=%async_computation | async-start | bytes 4718592 | tf_op jit(solution)/shard_map/all_to_all | solution.py:238
  648.4 57.2 %all-to-all-start.4 = ((bf16[32,32,1152]{2,1,0:T(8,128)(2,1)}), bf16[32,32,1152]{2,1,0:T(8,128)(2,1)S(1)}, u32[]{:S(2)}, u32[]{:S(2)}) async-start(bf16[32,32,1152]{2,1,0:T(8,128)(2,1)} %bitcast.214), calls=%async_computation.4 | async-start | bytes 4718592 | tf_op jit(solution)/shard_map/all_to_all | solution.py:261
  651.2 401.2 %reduce-scatter.17.cloned.1.call-start = ((), (), s32[]{:S(2)}) async-start(), calls=%async_computation.19 | async-start | bytes 5971968 | tf_op jit(solution)/shard_map/reduce_scatter | solution.py:304
  748.0 482.0 %reduce-scatter.15.cloned.1.call-start = ((), (), s32[]{:S(2)}) async-start(), calls=%async_computation.18 | async-start | bytes 17915904 | tf_op jit(solution)/shard_map/reduce_scatter | solution.py:303
  961.8 617.9 %reduce-scatter.21.cloned.1.call-start = ((), (), s32[]{:S(2)}) async-start(), calls=%async_computation.21 | async-start | bytes 23887872 | tf_op jit(solution)/shard_map/reduce_scatter | solution.py:306
  978.3 951.1 %reduce-scatter.19.cloned.1.call-start = ((), (), s32[]{:S(2)}) async-start(), calls=%async_computation.20 | async-start | bytes 23887872 | tf_op jit(solution)/shard_map/reduce_scatter | solution.py:305
  995.4 1025.6 %all-gather.19.cloned.1.call-start = ((), (), s32[]{:S(2)}) async-start(), calls=%async_computation.23 | async-start | bytes 3649536 | tf_op jit(solution)/shard_map/all_gather | solution.py:317
  1052.3 975.4 %reduce-scatter.27.cloned.1.call-start = ((), (), s32[]{:S(2)}) async-start(), calls=%async_computation.25 | async-start | bytes 1474560
  1054.9 1001.0 %reduce-scatter.25.cloned.1.call-start = ((), (), s32[]{:S(2)}) async-start(), calls=%async_computation.24 | async-start | bytes 2949120
  1233.1 860.6 %reduce-scatter.23.cloned.1.call-start = ((), (), s32[]{:S(2)}) async-start(), calls=%async_computation.22 | async-start | bytes 3317760 | tf_op jit(solution)/shard_map/reduce_scatter | solution.py:312
  1579.7 353.2 %copy-start.29 = (f32[4,576]{1,0:T(4,128)S(1)}, f32[4,576]{1,0:T(4,128)}, u32[]{:S(2)}) copy-start(f32[4,576]{1,0:T(4,128)} %copy-done.28) | copy-start | bytes 27652
  1579.7 353.2 %copy-start.31 = (f32[4,576]{1,0:T(4,128)S(1)}, f32[4,576]{1,0:T(4,128)}, u32[]{:S(2)}) copy-start(f32[4,576]{1,0:T(4,128)} %copy-done.30) | copy-start | bytes 27652
  1579.7 553.6 %reduce-scatter.29.cloned.1.call-start = ((), (), s32[]{:S(2)}) async-start(), calls=%async_computation.26 | async-start | bytes 3686400
  (81 other events, 978.2 us)
Sparse Core Ops, SparseCore 0:
  9.6 105.0 all-gather.8
  116.2 55.7 all-gather.10
  173.6 25.6 all-gather.12
  200.7 96.1 all-gather.14
  298.4 70.9 all-gather.16
  748.1 104.0 reduce-scatter.16
  961.9 268.0 reduce-scatter.14
  1233.9 345.7 reduce-scatter.20
  1583.5 345.7 reduce-scatter.18
  1932.7 59.8 all-gather.18
  1995.2 24.6 reduce-scatter.26
  2022.9 32.9 reduce-scatter.24
  2059.0 34.5 reduce-scatter.22
  2096.6 36.5 reduce-scatter.28
where the time goes:
time: 2150 us; the launch traced here: 2140 us
  waiting for transfers between devices  1110 us (52%)
  matrix products  469 us (22%)
  local copies, waits for them, and re-layouts  211 us (10%)
  blocking collectives  184 us (9%)
  other arithmetic  129 us (6%)
    reduce_scatter x1, waiting for transfers between devices, on_device(): lax.psum_scatter(weight_grads[2], 'seq', scatter_dimension=1, tiled=True)  350 us
    reduce_scatter x1, waiting for transfers between devices, on_device(): lax.psum_scatter(weight_grads[3], 'seq', scatter_dimension=1, tiled=True)  347 us
    reduce_scatter x1, waiting for transfers between devices, on_device(): lax.psum_scatter(weight_grads[0], 'seq', scatter_dimension=1, tiled=True)  175 us
    unnamed x17, waiting for transfers between devices  69.2 us
    dot_general x16, matrix products, attend_forward(): result = jnp.dot(attention, head_values, preferred_element_type=jnp.float32)  69.2 us
    dot_general x32, matrix products, masked_scores(): jnp.einsum('qe,ke->qk', head_queries, head_keys, preferred_element_type=j...  61.9 us
    all_to_all x1, blocking collectives, on_device(): lax.all_to_all(spread(owner_out), ('seq', 'mp'), split_axis=0, concat_axi...  59.9 us
    unnamed x157, local copies, waits for them, and re-layouts  56.5 us
  transfers between devices with their start and end apart: 18, of which 10 were waited for; matrix products, arithmetic and copies ran while one was open for 30% of the time, Pallas kernels for 0%

commit v1 on v0

v1 whole, which is shorter than its diff:
```python
import math

import jax
import jax.numpy as jnp
from jax import lax
from jax.sharding import PartitionSpec as P


HIGHEST = lax.Precision.HIGHEST
EVERY = ("seq", "mp")


def sinusoid(stamps, model_width):
    half_width = model_width // 2
    frequency = jnp.exp(
        -math.log(10000.0) * jnp.arange(half_width).astype(jnp.float32) / half_width
    )
    angles = stamps.astype(jnp.float32)[:, None] * frequency[None, :]
    return jnp.concatenate([jnp.cos(angles), jnp.sin(angles)], axis=1)


def norm_stats(values):
    center = values - jnp.mean(values, axis=-1, keepdims=True)
    inv = lax.rsqrt(jnp.mean(center * center, axis=-1, keepdims=True) + 1e-06)
    return center * inv, inv


def norm_back(kept, inv, normal):
    mean_kept = jnp.mean(kept, axis=-1, keepdims=True)
    mean_both = jnp.mean(kept * normal, axis=-1, keepdims=True)
    return inv * (kept - mean_kept - normal * mean_both)


def split_heads(values, head_count):
    row_count, model_width = values.shape
    return values.reshape(row_count, head_count, model_width // head_count).transpose(1, 0, 2)


def merge_heads(values):
    head_count, row_count, head_size = values.shape
    return values.transpose(1, 0, 2).reshape(row_count, head_count * head_size)


def masked_scores(head_queries, head_keys, same_item, score_scale):
    scores = (
        jnp.einsum("qe,ke->qk", head_queries, head_keys, preferred_element_type=jnp.float32)
        * score_scale
    )
    return jnp.where(same_item, scores, -1e30)


def attend_forward(triple, same_item, score_scale):
    head_queries, head_keys, head_values = triple
    scores = masked_scores(head_queries, head_keys, same_item, score_scale)
    row_max = jnp.max(scores, axis=1, keepdims=True)
    exp_scores = jnp.exp(scores - row_max)
    row_total = jnp.sum(exp_scores, axis=1, keepdims=True)
    attention = (exp_scores / row_total).astype(jnp.bfloat16)
    result = jnp.dot(attention, head_values, preferred_element_type=jnp.float32)
    return (result, (row_max + jnp.log(row_total))[:, 0])


def attend_backward(quintet, same_item, score_scale):
    head_queries, head_keys, head_values, head_grad, log_total = quintet
    scores = masked_scores(head_queries, head_keys, same_item, score_scale)
    probs_full = jnp.exp(scores - log_total[:, None])
    attention = probs_full.astype(jnp.bfloat16)
    grad_soft = jnp.einsum("qe,ke->qk", head_grad, head_values, preferred_element_type=jnp.float32)
    row_inner = jnp.sum(grad_soft * probs_full, axis=1, keepdims=True)
    grad_scores = (probs_full * (grad_soft - row_inner)).astype(jnp.bfloat16)
    grad_queries = jnp.dot(grad_scores, head_keys, preferred_element_type=jnp.float32) * score_scale
    grad_keys = (
        jnp.einsum("qk,qe->ke", grad_scores, head_queries, preferred_element_type=jnp.float32)
        * score_scale
    )
    grad_values = jnp.einsum("qk,qe->ke", attention, head_grad, preferred_element_type=jnp.float32)
    return (grad_queries, grad_keys, grad_values)


def swap(values, axis_name, bit):
    size = lax.axis_size(axis_name)
    return lax.ppermute(values, axis_name, [(i, i ^ bit) for i in range(size)])


def pick(values, dim, major, index):
    shape = values.shape
    inner = shape[dim] // (2 * major)
    cut = values.reshape(shape[:dim] + (major, 2, inner) + shape[dim + 1 :])
    cut = lax.dynamic_index_in_dim(cut, index, dim + 1, keepdims=False)
    return cut.reshape(shape[:dim] + (major * inner,) + shape[dim + 1 :])


def halve(values, dim, axis_name, level, bits):
    mine = (lax.axis_index(axis_name) >> level) & 1
    major = 2 ** bits.index(level)
    sent = pick(values, dim, major, 1 - mine).astype(jnp.bfloat16)
    came = swap(sent, axis_name, 1 << level)
    kept = pick(values, dim, major, mine)
    bits.remove(level)
    return kept.astype(jnp.float32) + came.astype(jnp.float32)


def levels_of(axis_name):
    return list(range(lax.axis_size(axis_name).bit_length() - 1))[::-1]


def grad_sum(split_side, whole_side, split_first):
    mp_bits = levels_of("mp")
    seq_bits = levels_of("seq")
    core = lax.axis_index("mp") & 1
    major = 2 ** mp_bits.index(0)

    def product(side):
        if split_first:
            return jnp.einsum("nd,ne->de", side, whole_side, preferred_element_type=jnp.float32)
        return jnp.einsum("ne,nd->ed", whole_side, side, preferred_element_type=jnp.float32)

    sent = product(pick(split_side, 1, major, 1 - core)).astype(jnp.bfloat16)
    came = swap(sent, "mp", 1)
    kept = product(pick(split_side, 1, major, core))
    total = kept + came.astype(jnp.float32)
    mp_bits.remove(0)
    mp_dim = 0 if split_first else 1
    for level in mp_bits[::-1]:
        total = halve(total.astype(jnp.bfloat16), mp_dim, "mp", level, mp_bits)
    order = [level for level in seq_bits[::-1] if level != 0] + [0]
    for level in order:
        total = halve(total.astype(jnp.bfloat16), 1 - mp_dim, "seq", level, seq_bits)
    return total if split_first else total.T


def gelu_parts(pre):
    inner = math.sqrt(2.0 / math.pi)
    square = pre * pre
    bend = jnp.tanh(inner * (pre + 0.044715 * pre * square))
    value = 0.5 * pre * (1.0 + bend)
    slope = 0.5 * (1.0 + bend) + 0.5 * pre * (1.0 - bend * bend) * inner * (
        1.0 + 3.0 * 0.044715 * square
    )
    return value, slope


def on_device(
    tokens,
    cotangent,
    segment,
    timestep,
    head_mask,
    chan_mask,
    router_keep,
    ada_weight,
    ada_bias,
    qkv_weight,
    qv_bias,
    proj_weight,
    proj_bias,
    up_weight,
    up_bias,
    down_weight,
    down_bias,
):
    row_count, model_width = tokens.shape
    slot_count = timestep.shape[0]
    head_count = head_mask.shape[1]
    group_count = chan_mask.shape[1]
    hidden_width = up_bias.shape[0]
    score_scale = (model_width // head_count) ** (-0.5)
    mp_size = lax.axis_size("mp")
    seq_size = lax.axis_size("seq")
    slot_rows = row_count // slot_count
    blocked = (slot_count, slot_rows, model_width)
    flat = (row_count, model_width)
    single = segment[row_count - 1] == 0

    row_width = model_width // mp_size
    first_col = lax.axis_index("mp") * row_width

    def condition_of(stamps):
        value = jax.nn.silu(sinusoid(stamps, model_width)).astype(jnp.bfloat16)
        return lax.dynamic_slice_in_dim(value, first_col, row_width, 1)

    stamp_float = timestep.astype(jnp.float32)
    peer_stamps = [stamp_float] + [swap(stamp_float, "mp", k) for k in range(1, mp_size)]
    group_cond = condition_of(jnp.concatenate(peer_stamps))
    group_mod = jnp.dot(group_cond, ada_weight, preferred_element_type=jnp.float32)
    group_mod = group_mod.reshape(mp_size, slot_count, 6 * model_width)
    modulation = group_mod[0] + ada_bias.astype(jnp.float32)
    for k in range(1, mp_size):
        modulation = modulation + swap(group_mod[k], "mp", k)

    full_qkv = lax.all_gather(qkv_weight, "mp", axis=0, tiled=True)
    full_proj = lax.all_gather(proj_weight, "mp", axis=0, tiled=True)
    full_up = lax.all_gather(up_weight, "mp", axis=0, tiled=True)
    full_down = lax.all_gather(down_weight, "mp", axis=0, tiled=True)

    slot_mod = jnp.where(single, modulation[:1], modulation)
    first_shift, first_scale, first_gate, second_shift, second_scale, second_gate = [
        slot_mod[:, None, section * model_width : (section + 1) * model_width]
        for section in range(6)
    ]
    head_gate = jnp.where(single, head_mask[:1], head_mask).astype(jnp.float32)
    head_rows = jnp.repeat(head_gate, slot_rows, axis=0)
    chan_gate = jnp.where(single, chan_mask[:1], chan_mask).astype(jnp.float32)
    unit_gate = jnp.repeat(chan_gate, hidden_width // group_count, axis=1)[:, None, :]
    keep_rows = router_keep.astype(jnp.float32).reshape(slot_count, slot_rows, 1)

    tok_float = tokens.astype(jnp.float32).reshape(blocked)
    first_normal, first_inv = norm_stats(tok_float)
    normed = (first_normal * (1.0 + first_scale) + first_shift).astype(jnp.bfloat16).reshape(flat)
    joined = jnp.dot(normed, full_qkv, preferred_element_type=jnp.float32)
    qv_float = qv_bias.astype(jnp.float32)
    queries = (joined[:, :model_width] + qv_float[:model_width]).astype(jnp.bfloat16)
    keys_all = joined[:, model_width : 2 * model_width].astype(jnp.bfloat16)
    values_all = (joined[:, 2 * model_width :] + qv_float[model_width:]).astype(jnp.bfloat16)
    same_item = segment[:, None] == segment[None, :]
    head_inputs = (
        split_heads(queries, head_count),
        split_heads(keys_all, head_count),
        split_heads(values_all, head_count),
    )
    attended, log_total = lax.map(
        lambda triple: attend_forward(triple, same_item, score_scale), head_inputs
    )
    attn_cat = merge_heads(attended * head_rows.T[:, :, None]).astype(jnp.bfloat16)
    branch = jnp.dot(attn_cat, full_proj, preferred_element_type=jnp.float32) + proj_bias.astype(
        jnp.float32
    )
    branch = branch.reshape(blocked)
    middle = tok_float + first_gate * branch
    second_normal, second_inv = norm_stats(middle)
    second_in = (second_normal * (1.0 + second_scale) + second_shift).astype(jnp.bfloat16)
    second_in = second_in.reshape(flat)

    pre_act = jnp.dot(second_in, full_up, preferred_element_type=jnp.float32) + up_bias.astype(
        jnp.float32
    )
    value, slope = gelu_parts(pre_act.reshape(slot_count, slot_rows, hidden_width))
    hidden = (value * unit_gate).astype(jnp.bfloat16).reshape(row_count, hidden_width)
    mlp_out = (
        jnp.dot(hidden, full_down, preferred_element_type=jnp.float32)
        + down_bias.astype(jnp.float32)
    ).astype(jnp.bfloat16)
    mlp_float = mlp_out.astype(jnp.float32).reshape(blocked)
    output = (middle + keep_rows * second_gate * mlp_float).astype(jnp.bfloat16).reshape(flat)

    grad_final = cotangent.astype(jnp.float32).reshape(blocked)
    grad_out = (keep_rows * second_gate * grad_final).astype(jnp.bfloat16).reshape(flat)
    grad_second_gate = jnp.sum(keep_rows * grad_final * mlp_float, axis=1)
    grad_hidden = jnp.einsum(
        "nd,fd->nf", grad_out, full_down, preferred_element_type=jnp.float32
    ).reshape(slot_count, slot_rows, hidden_width)
    grad_pre = (grad_hidden * unit_gate * slope).astype(jnp.bfloat16)
    grad_pre = grad_pre.reshape(row_count, hidden_width)
    down_piece = grad_sum(hidden, grad_out, False)
    grad_second = (
        jnp.einsum("nf,df->nd", grad_pre, full_up, preferred_element_type=jnp.float32)
        .astype(jnp.bfloat16)
        .astype(jnp.float32)
        .reshape(blocked)
    )
    up_piece = grad_sum(second_in, grad_pre, True)
    up_bias_grad = jnp.sum(grad_pre.astype(jnp.float32), axis=0)
    down_bias_grad = jnp.sum(grad_out.astype(jnp.float32), axis=0)

    grad_second_scale = jnp.sum(grad_second * second_normal, axis=1)
    grad_second_shift = jnp.sum(grad_second, axis=1)
    grad_middle = grad_final + norm_back(
        grad_second * (1.0 + second_scale), second_inv, second_normal
    )
    grad_branch = (first_gate * grad_middle).astype(jnp.bfloat16).reshape(flat)
    grad_first_gate = jnp.sum(grad_middle * branch, axis=1)
    grad_cat = jnp.einsum(
        "ne,de->nd", grad_branch, full_proj, preferred_element_type=jnp.float32
    ).astype(jnp.bfloat16)
    proj_piece = grad_sum(attn_cat, grad_branch, False)
    proj_bias_grad = jnp.sum(grad_branch.astype(jnp.float32), axis=0)

    lone = jnp.arange(slot_count)[:, None] == 0

    def per_item(sums):
        return jnp.where(single, jnp.where(lone, jnp.sum(sums, axis=0, keepdims=True), 0.0), sums)

    early = per_item(
        jnp.concatenate(
            [grad_first_gate, grad_second_shift, grad_second_scale, grad_second_gate], axis=1
        )
    )
    rest = jnp.zeros((early.shape[1] - 2 * model_width - slot_count,), jnp.float32)
    early_rows = jnp.concatenate(
        [
            early,
            up_bias_grad[None, :],
            jnp.concatenate([down_bias_grad, proj_bias_grad, stamp_float, rest])[None, :],
        ],
        axis=0,
    )
    all_early = lax.all_gather(early_rows, EVERY, axis=0, tiled=False)
    grad_heads = split_heads(grad_cat, head_count) * head_rows.T[:, :, None].astype(jnp.bfloat16)
    grad_queries, grad_keys, grad_values = lax.map(
        lambda quintet: attend_backward(quintet, same_item, score_scale),
        head_inputs + (grad_heads, log_total),
    )
    grad_joined = jnp.concatenate(
        [merge_heads(grad_queries), merge_heads(grad_keys), merge_heads(grad_values)], axis=1
    ).astype(jnp.bfloat16)
    grad_normed = jnp.einsum("ne,de->nd", grad_joined, full_qkv, preferred_element_type=jnp.float32)
    qkv_piece = grad_sum(normed, grad_joined, False)
    column_sums = jnp.sum(grad_joined.astype(jnp.float32), axis=0)
    qv_bias_grad = jnp.concatenate([column_sums[:model_width], column_sums[2 * model_width :]])
    grad_normed = grad_normed.reshape(blocked)
    token_grad = grad_middle + norm_back(
        grad_normed * (1.0 + first_scale), first_inv, first_normal
    )
    grad_first_scale = jnp.sum(grad_normed * first_normal, axis=1)
    grad_first_shift = jnp.sum(grad_normed, axis=1)
    late = per_item(jnp.concatenate([grad_first_shift, grad_first_scale], axis=1))
    late_rows = jnp.concatenate([late, qv_bias_grad[None, :]], axis=0)
    all_late = lax.all_gather(late_rows, EVERY, axis=0, tiled=False)

    item_count = slot_count * mp_size * seq_size
    all_modulation = jnp.concatenate(
        [all_late[:, :slot_count], all_early[:, :slot_count]], axis=2
    ).reshape(item_count, 6 * model_width)
    all_stamps = all_early[:, slot_count + 1, 2 * model_width : 2 * model_width + slot_count]
    cond_cols = condition_of(all_stamps.reshape(item_count)).astype(jnp.float32)
    col_width = 6 * model_width // seq_size
    mod_cols = lax.dynamic_slice_in_dim(
        all_modulation, lax.axis_index("seq") * col_width, col_width, 1
    )
    ada_piece = jnp.einsum("sd,sc->dc", cond_cols, mod_cols, precision=HIGHEST)
    ada_bias_grad = jnp.sum(all_modulation, axis=0)
    early_bias = jnp.sum(all_early[:, slot_count:], axis=0)
    return (
        output,
        token_grad.reshape(flat),
        ada_piece,
        qkv_piece,
        proj_piece,
        up_piece,
        down_piece.reshape(hidden_width // mp_size, model_width // seq_size),
        ada_bias_grad,
        jnp.sum(all_late[:, slot_count], axis=0),
        early_bias[1, model_width : 2 * model_width],
        early_bias[0],
        early_bias[1, :model_width],
    )


def solution(mesh):
    in_specs = (
        P(("seq", "mp"), None),
        P(("seq", "mp"), None),
        P(("seq", "mp")),
        P(("seq", "mp")),
        P(("seq", "mp"), None),
        P(("seq", "mp"), None),
        P(("seq", "mp")),
        P("mp", None),
        P(),
        P("mp", None),
        P(),
        P("mp", None),
        P(),
        P("mp", None),
        P(),
        P("mp", None),
        P(),
    )
    out_specs = (
        P(("seq", "mp"), None),
        P(("seq", "mp"), None),
        P("mp", "seq"),
        P("mp", "seq"),
        P("mp", "seq"),
        P("mp", "seq"),
        P("mp", "seq"),
        P(),
        P(),
        P(),
        P(),
        P(),
    )
    return jax.shard_map(
        on_device, mesh=mesh, in_specs=in_specs, out_specs=out_specs, check_vma=False
    )
```

time: 2150 us -> 1230 us (0.57)
  waiting for transfers between devices: 1110 us -> 141 us
  blocking collectives: 184 us -> 0 us
  local copies, waits for them, and re-layouts: 211 us -> 393 us
  other arithmetic: 129 us -> 179 us
    reduce_scatter x5 -> x0, waiting for transfers between devices: 909 us -> none  [the longest x1 350 us: on_device(): lax.psum_scatter(weight_grads[2], 'seq', scatter_dimension=1, tiled=True)]
    ppermute x0 -> x26, waiting for transfers between devices: none -> 139 us  [swap(): return lax.ppermute(values, axis_name, [(i, i ^ bit) for i in range(size)])]
    reshape x2 -> x21, local copies, waits for them, and re-layouts: 0.32 us -> 94.8 us  [the longest x2 50.3 us: on_device(): pre_act.reshape(slot_count, slot_rows, hidden_width)]
    convert_element_type x6 -> x27, other arithmetic: 8.24 us -> 88.4 us  [the longest x12 24.2 us: grad_sum(): total.astype(jnp.bfloat16)]
    mul x2 -> x12, local copies, waits for them, and re-layouts: 21.3 us -> 92 us  [the longest x4 59.1 us: on_device(): value * unit_gate]
    all_gather x6, waiting for transfers between devices: 70.1 us -> 0.03 us  [the longest x1 0.02 us: on_device(): all_early = lax.all_gather(early_rows, EVERY, axis=0, tiled=False)]
    unnamed x17 -> x6, waiting for transfers between devices: 69.2 us -> 2.11 us
    all_to_all x4 -> x0, waiting for transfers between devices: 62.7 us -> none  [the longest x1 42.1 us: on_device(): lax.all_to_all(spread(owner_back), ('seq', 'mp'), split_axis=0, concat_ax...]
  transfers between devices with their start and end apart: 18 -> 32, of which waited for: 10 -> 11; matrix products, arithmetic and copies ran while one was open for 30% -> 58% of each run, Pallas kernels for 0% -> 0%
where the time goes in v1:
time: 1230 us; the launch traced here: 1220 us
  matrix products  460 us (37%)
  local copies, waits for them, and re-layouts  393 us (32%)
  other arithmetic  179 us (15%)
  waiting for transfers between devices  141 us (11%)
  starting transfers between devices  28.3 us (2%)
  between operations  16.3 us (1%)
    ppermute x26, waiting for transfers between devices, swap(): return lax.ppermute(values, axis_name, [(i, i ^ bit) for i in range(size)])  139 us
    dot_general x32, matrix products, masked_scores(): jnp.einsum('qe,ke->qk', head_queries, head_keys, preferred_element_type=j...  61.7 us
    mul x4, local copies, waits for them, and re-layouts, on_device(): value * unit_gate  59.1 us
    dynamic_slice x11, local copies, waits for them, and re-layouts, pick(): cut = lax.dynamic_index_in_dim(cut, index, dim + 1, keepdims=False)  57 us
    reshape x2, local copies, waits for them, and re-layouts, on_device(): pre_act.reshape(slot_count, slot_rows, hidden_width)  50.3 us
    dot_general x16, matrix products, attend_forward(): result = jnp.dot(attention, head_values, preferred_element_type=jnp.float32)  48.3 us
    unnamed x183, local copies, waits for them, and re-layouts  43 us
    dot_general x6, matrix products, product(): jnp.einsum('ne,nd->ed', whole_side, side, preferred_element_type=jnp.floa...  42.5 us
  transfers between devices with their start and end apart: 32, of which 11 were waited for; matrix products, arithmetic and copies ran while one was open for 58% of the time, Pallas kernels for 0%

profile of v1, /device:TPU:0, one launch (start us, length us, event | category | flops | bytes accessed | tf_op | source)
XLA Modules:
  0.0 1218.3 jit_solution(8348078279727320356)
XLA Ops:
  41.9 21.9 %mul.528 = f32[1024,2,2,1152]{3,2,1,0:T(2,128)} reshape(f32[4,256,4608]{2,1,0:T(8,128)} %mul.456) | data formatting | bytes 37748736 | tf_op jit(solution)/shard_map/mul | solution.py:238
  63.7 28.2 %copy.297 = f32[1024,2,2,1152]{0,3,1,2:T(8,128)} copy(f32[1024,2,2,1152]{3,2,1,0:T(2,128)} %mul.528) | data formatting | bytes 37748736 | tf_op jit(solution)/shard_map/mul | solution.py:238
  171.2 13.0 %fusion.115 = f32[1024,3456]{1,0:T(8,128)S(1)} fusion(bf16[1024,1152]{1,0:T(8,128)(2,1)} %fusion.59, bf16[1152,3456]{1,0:T(8,128)(2,1)} %all-gather.11.cloned.1.call-done), kind=kOutput, calls=%fused_computation.269 | convolution fusion | flops 8153726976 | bytes 24477696 | tf_op jit(solution)/shard_map/dot_general | solution.py:210
  219.1 116.0 %while.30 = (s32[]{:T(128)}, f32[16,1024,72]{1,2,0:T(8,128)}, f32[16,1024]{1,0:T(8,128)}, bf16[16,1024,72]{2,1,0:T(8,128)(2,1)}, bf16[16,1024,72]{2,1,0:T(8,128)...) while((s32[]{:T(128)}, f32[16,1024,72]{1,2,0:T(8,128)}, ...), condition=%wide.region_5.6_spmd.clone.clone, body=%wide.region_2.5_spmd.clone.sunk.clone | while | flops 317717504 | bytes 13727833 | solution.py:221
  359.0 12.7 %add_convert_fusion.3 = (bf16[1024,2,2,288]{0,3,2,1:T(8,128)(2,1)S(1)}, bf16[1024,2,2,288]{0,3,2,1:T(8,128)(2,1)S(1)}) fusion(f32[1024,2,2,288]{0,3,2,1:T(8,128)} %add.417, f32[1024,2,2,288]{0,3,2,1:T(8,128)} %mul.519, f32[1024,2,2,288]{0,3,2,1:T(8,128)} %bitcast.402, f32[1024,2,2,288]{0,3,2,1:T(8,128)} %mul.515, f32[1024,2,2,288]{0,3,2,1:T(8,128)} %bitcast.403, ...), kind=kLoop, calls=%fused_computation.105 | loop fusion | flops 14155776 | bytes 37765120 | tf_op jit(solution)/shard_map/convert_element_type | solution.py:231
  377.6 23.7 %fusion.52 = (bf16[1024,4608]{1,0:T(8,128)(2,1)}, f32[1024,4608]{1,0:T(8,128)}) fusion(f32[4,4608]{1,0:T(4,128)S(1)} %copy-done.25, f32[4608]{0:T(1024)S(1)} %copy-done.48, bf16[1024,1152]{1,0:T(8,128)(2,1)S(1)} %fusion.61, bf16[1152,4608]{1,0:T(8,128)(2,1)} %all-gather.15.cloned.1.call-done), kind=kOutput, calls=%fused_computation.57 | convolution fusion | flops 10923540480 | bytes 41379840 | tf_op jit(solution)/shard_map/dot_general | solution.py:234
  401.4 22.0 %reshape.628 = f32[1024,2,2,1152]{3,2,1,0:T(2,128)} reshape(f32[1024,4608]{1,0:T(8,128)} %get-tuple-element.360) | data formatting | bytes 37748736 | tf_op jit(solution)/shard_map/reshape | solution.py:237
  423.4 27.1 %convert_reduce_fusion = (f32[4608]{0:T(1024)}, bf16[4,256,4608]{2,1,0:T(8,128)(2,1)}) fusion(f32[4,256,4608]{2,1,0:T(8,128)} %bitcast.399, f32[4,4608]{1,0:T(4,128)S(1)} %copy-done.25, bf16[4,256,1152]{2,1,0:T(8,128)(2,1)S(1)} %bitcast.426, bf16[4608,1152]{1,0:T(8,128)(2,1)} %all-gather.17.cloned.1.call-done), kind=kOutput, calls=%fused_computation.59 | convolution fusion | flops 10970722304 | bytes 41379840 | tf_op jit(solution)/shard_map/nd,fd->nf/dot_general | solution.py:249
  450.5 20.3 %fusion.72 = (f32[1024]{0:T(1024)S(1)}, f32[1024]{0:T(1024)S(1)}, bf16[1024,1152]{1,0:T(8,128)(2,1)}) fusion(f32[4,1152]{1,0:T(4,128)S(1)} %copy-done.30, f32[1024]{0:T(1024)S(1)} %add_rsqrt_fusion, f32[1024,1152]{1,0:T(8,128)} %copy-done.2, f32[1024]{0:T(1024)S(1)} %broadcast_multiply_fusion.5, bf16[1024,4608]{1,0:T(8,128)(2,1)} %bitcast.447, ...), kind=kOutput, calls=%fused_computation.124 | convolution fusion | flops 10881071104 | bytes 27166720 | tf_op jit(solution)/shard_map/nf,df->nd/dot_general | solution.py:256
  472.0 24.2 %convert_reduce_fusion.2 = (f32[1152]{0:T(1024)S(1)}, bf16[1024,1152]{1,0:T(8,128)(2,1)}, f32[1024,1152]{1,0:T(8,128)}, bf16[1024,1152]{1,0:T(8,128)(2,1)}, f32[1024,1152]{1,0:T(8,128)}) fusion(f32[4,1152]{1,0:T(4,128)S(1)} %copy-done.28, f32[1024]{0:T(1024)S(1)} %broadcast_multiply_fusion.3, f32[1024,1152]{1,0:T(8,128)} %copy-done.2, ...), kind=kOutput, calls=%fused_computation.107 | convolution fusion | flops 10896407552 | bytes 43731968 | tf_op jit(solution)/shard_map/dot_general | solution.py:240
  507.2 202.5 %while.31 = (s32[]{:T(128)}, bf16[16,1024,72]{1,2,0:T(8,128)(2,1)}, bf16[16,1024,72]{1,2,0:T(8,128)(2,1)}, bf16[16,1024,72]{1,2,0:T(8,128)(2,1)}, bf16[16,1024,7...) while((s32[]{:T(128)}, bf16[16,1024,72]{1,2,0:T(8,128)(2,1)}, ...), condition=%wide.region_12.13_spmd.clone.clone, body=%wide.region_10.12_spmd.clone.sunk.clone | while | flops 765606912 | bytes 33981552 | solution.py:299
  714.7 17.1 %fusion.71 = (f32[1024]{0:T(1024)}, f32[1024]{0:T(1024)}, f32[1024,1152]{1,0:T(8,128)}) fusion(f32[4,1152]{1,0:T(4,128)S(1)} %copy-done.35, f32[1024]{0:T(1024)S(1)} %copy-done.47, f32[1024]{0:T(1024)S(1)} %copy-done.44, bf16[1024,1152]{1,0:T(8,128)(2,1)S(1)} %copy-done.1, bf16[1152,3456]{1,0:T(8,128)(2,1)} %all-gather.11.cloned.1.call-done, ...), kind=kOutput, calls=%fused_computation.123 | convolution fusion | flops 8183216128 | bytes 22153216 | tf_op jit(solution)/shard_map/ne,de->nd/dot_general | solution.py:306
  755.4 11.0 convolution_convert_fusion.1
  766.5 28.2 %copy.292 = f32[1024,2,2,1152]{0,3,1,2:T(8,128)} copy(f32[1024,2,2,1152]{3,2,1,0:T(2,128)} %reshape.628) | data formatting | bytes 37748736 | tf_op jit(solution)/shard_map/reshape | solution.py:237
  794.7 17.8 %multiply_convert_fusion.1 = bf16[1024,2,2,1152]{0,3,1,2:T(8,128)(2,1)} fusion(f32[1024,2,2,1152]{0,3,1,2:T(8,128)} %copy.297, f32[1024,2,2,1152]{0,3,1,2:T(8,128)} %copy.292), kind=kLoop, calls=%fused_computation.58 | loop fusion | flops 47185920 | bytes 47185920 | tf_op jit(solution)/shard_map/convert_element_type | solution.py:238
  835.4 15.2 %collective-permute-done.12 = bf16[1152,288]{0,1:T(8,128)(2,1)} collective-permute-done((bf16[1152,288]{0,1:T(8,128)(2,1)S(1)}, bf16[1152,288]{0,1:T(8,128)(2,1)}, u32[]{:S(2)}, u32[]{:S(2)}) %collective-permute-start.12) | collective-permute-done | bytes 663584 | tf_op jit(solution)/shard_map/ppermute | solution.py:82
  913.8 11.8 add_convert_fusion.1
  939.6 11.0 reshape.631
  950.6 19.2 %collective-permute-done.7 = bf16[3456,288]{0,1:T(8,128)(2,1)S(1)} collective-permute-done((bf16[3456,288]{0,1:T(8,128)(2,1)}, bf16[3456,288]{0,1:T(8,128)(2,1)S(1)}, u32[]{:S(2)}, u32[]{:S(2)}) %collective-permute-start.7) | collective-permute-done | bytes 1990688 | tf_op jit(solution)/shard_map/ppermute | solution.py:82
  988.7 14.0 %constant_dynamic-slice_fusion.4 = (bf16[1152,1,1,1152]{3,2,0,1:T(2,128)(2,1)}, bf16[1152,1,1,1152]{3,2,0,1:T(2,128)(2,1)S(1)}) fusion(bf16[1152,1,2,1152]{3,2,0,1:T(2,128)(2,1)} %reshape.631, s32[]{:T(128)S(6)} %select_n.151, s32[]{:T(128)S(6)} %select_n.152), kind=kLoop, calls=%fused_computation.221 | loop fusion | bytes 10616840 | tf_op jit(solution)/shard_map/jit(dynamic_index_in_dim)/dynamic_slice | solution.py:89
  1053.2 10.9 collective-permute-done.9
  1068.0 14.2 %collective-permute-done.22 = bf16[1152,1152]{1,0:T(8,128)(2,1)} collective-permute-done((bf16[1152,1152]{1,0:T(8,128)(2,1)}, bf16[1152,1152]{1,0:T(8,128)(2,1)}, u32[]{:S(2)}, u32[]{:S(2)}) %collective-permute-start.22) | collective-permute-done | bytes 2654240 | tf_op jit(solution)/shard_map/ppermute | solution.py:82
  1131.3 29.3 %collective-permute-done.18 = bf16[288,2304]{1,0:T(8,128)(2,1)} collective-permute-done((bf16[288,2304]{1,0:T(8,128)(2,1)}, bf16[288,2304]{1,0:T(8,128)(2,1)}, u32[]{:S(2)}, u32[]{:S(2)}) %collective-permute-start.18) | collective-permute-done | bytes 1327136 | tf_op jit(solution)/shard_map/ppermute | solution.py:82
  1173.3 26.0 %collective-permute-done.19 = bf16[288,1152]{1,0:T(8,128)(2,1)S(1)} collective-permute-done((bf16[288,1152]{1,0:T(8,128)(2,1)S(1)}, bf16[288,1152]{1,0:T(8,128)(2,1)S(1)}, u32[]{:S(2)}, u32[]{:S(2)}) %collective-permute-start.19) | collective-permute-done | bytes 663584 | tf_op jit(solution)/shard_map/ppermute | solution.py:82
  (601 shorter events, 781.9 us)
Async XLA Ops:
  7.2 164.0 %all-gather.11.cloned.1.call-start = ((), (), s32[]{:S(2)}) async-start(), calls=%async_computation | async-start | bytes 9953280 | tf_op jit(solution)/shard_map/all_gather | solution.py:191
  7.9 331.6 %all-gather.13.cloned.1.call-start = ((), (), s32[]{:S(2)}) async-start(), calls=%async_computation.1 | async-start | bytes 3317760 | tf_op jit(solution)/shard_map/all_gather | solution.py:192
  8.7 369.0 %all-gather.15.cloned.1.call-start = ((), (), s32[]{:S(2)}) async-start(), calls=%async_computation.2 | async-start | bytes 13271040 | tf_op jit(solution)/shard_map/all_gather | solution.py:193
  9.4 414.0 %all-gather.17.cloned.1.call-start = ((), (), s32[]{:S(2)}) async-start(), calls=%async_computation.3 | async-start | bytes 13271040 | tf_op jit(solution)/shard_map/all_gather | solution.py:194
  9.5 82.5 %collective-permute-start.2 = (f32[4]{0:T(128)S(1)}, f32[4]{0:T(128)S(1)}, u32[]{:S(2)}, u32[]{:S(2)}) collective-permute-start(f32[4]{0:T(128)S(1)} %convert_element_type.366), channel_id=1, source_target_pairs={{0,3},{1,2},{2,1},{3,0},{4,7},{5,6},{6,5},{7,4},{8,11},{9,10},{10,... | collective-permute-start | bytes 56 | tf_op jit(solution)/shard_map/ppermute | solution.py:82
  12.0 80.0 %collective-permute-start.1 = (f32[4]{0:T(128)S(1)}, f32[4]{0:T(128)S(1)}, u32[]{:S(2)}, u32[]{:S(2)}) collective-permute-start(f32[4]{0:T(128)S(1)} %convert_element_type.366), channel_id=1, source_target_pairs={{0,2},{1,3},{2,0},{3,1},{4,6},{5,7},{6,4},{7,5},{8,10},{9,11},{10,... | collective-permute-start | bytes 56 | tf_op jit(solution)/shard_map/ppermute | solution.py:82
  12.6 79.4 %collective-permute-start = (f32[4]{0:T(128)S(1)}, f32[4]{0:T(128)S(1)}, u32[]{:S(2)}, u32[]{:S(2)}) collective-permute-start(f32[4]{0:T(128)S(1)} %convert_element_type.366), channel_id=1, source_target_pairs={{0,1},{1,0},{2,3},{3,2},{4,5},{5,4},{6,7},{7,6},{8,9},{9,8},{10,11... | collective-permute-start | bytes 56 | tf_op jit(solution)/shard_map/ppermute | solution.py:82
  12.7 884.7 %all-gather.21.cloned.1.call-start = ((), (), s32[]{:S(2)}) async-start(), calls=%async_computation.5 | async-start | bytes 2433024 | tf_op jit(solution)/shard_map/all_gather | solution.py:318
  742.5 275.7 %all-gather.19.cloned.1.call-start = ((), (), s32[]{:S(2)}) async-start(), calls=%async_computation.4 | async-start | bytes 4866048 | tf_op jit(solution)/shard_map/all_gather | solution.py:297
  752.1 150.8 %collective-permute-start.6 = (bf16[3456,576]{0,1:T(8,128)(2,1)}, bf16[3456,576]{0,1:T(8,128)(2,1)}, u32[]{:S(2)}, u32[]{:S(2)}) collective-permute-start(bf16[3456,576]{0,1:T(8,128)(2,1)} %convolution_convert_fusion.2), channel_id=1, source_target_pairs={{0,1},{1,0},{2,3},{3,2},{4,5},{5,4},{6,7},{7,6},{8,9},{9,8},{10,11... | collective-permute-start | bytes 11943944 | tf_op jit(solution)/shard_map/ppermute | solution.py:82
  754.9 74.1 %collective-permute-start.11 = (bf16[1152,576]{0,1:T(8,128)(2,1)}, bf16[1152,576]{0,1:T(8,128)(2,1)}, u32[]{:S(2)}, u32[]{:S(2)}) collective-permute-start(bf16[1152,576]{0,1:T(8,128)(2,1)} %convolution_convert_fusion.5), channel_id=1, source_target_pairs={{0,1},{1,0},{2,3},{3,2},{4,5},{5,4},{6,7},{7,6},{8,9},{9,8},{10,11... | collective-permute-start | bytes 3981320 | tf_op jit(solution)/shard_map/ppermute | solution.py:82
  766.4 147.4 %collective-permute-start.16 = (bf16[576,4608]{1,0:T(8,128)(2,1)}, bf16[576,4608]{1,0:T(8,128)(2,1)}, u32[]{:S(2)}, u32[]{:S(2)}) collective-permute-start(bf16[576,4608]{1,0:T(8,128)(2,1)} %convolution_convert_fusion.1), channel_id=1, source_target_pairs={{0,1},{1,0},{2,3},{3,2},{4,5},{5,4},{6,7},{7,6},{8,9},{9,8},{10,11... | collective-permute-start | bytes 15925256 | tf_op jit(solution)/shard_map/ppermute | solution.py:82
  834.9 95.7 %collective-permute-start.21 = (bf16[1152,2304]{1,0:T(8,128)(2,1)}, bf16[1152,2304]{1,0:T(8,128)(2,1)}, u32[]{:S(2)}, u32[]{:S(2)}) collective-permute-start(bf16[1152,2304]{1,0:T(8,128)(2,1)} %convolution_convert_fusion), channel_id=1, source_target_pairs={{0,1},{1,0},{2,3},{3,2},{4,5},{5,4},{6,7},{7,6},{8,9},{9,8},{10,11... | collective-permute-start | bytes 15925256 | tf_op jit(solution)/shard_map/ppermute | solution.py:82
  913.2 56.6 %collective-permute-start.7 = (bf16[3456,288]{0,1:T(8,128)(2,1)}, bf16[3456,288]{0,1:T(8,128)(2,1)S(1)}, u32[]{:S(2)}, u32[]{:S(2)}) collective-permute-start(bf16[3456,288]{0,1:T(8,128)(2,1)} %dynamic-slice_bitcast_fusion.1), channel_id=1, source_target_pairs={{0,2},{1,3},{2,0},{3,1},{4,6},{5,7},{6,4},{7,5},{8,10},{9,11},{10,... | collective-permute-start | bytes 5971976 | tf_op jit(solution)/shard_map/ppermute | solution.py:82
  929.9 158.8 %collective-permute-start.17 = (bf16[288,4608]{1,0:T(8,128)(2,1)}, bf16[288,4608]{1,0:T(8,128)(2,1)}, u32[]{:S(2)}, u32[]{:S(2)}) collective-permute-start(bf16[288,4608]{1,0:T(8,128)(2,1)} %dynamic-slice_bitcast_fusion), channel_id=1, source_target_pairs={{0,2},{1,3},{2,0},{3,1},{4,6},{5,7},{6,4},{7,5},{8,10},{9,11},{10,... | collective-permute-start | bytes 7962632 | tf_op jit(solution)/shard_map/ppermute | solution.py:82
  988.2 40.3 %collective-permute-start.8 = (bf16[1728,288]{0,1:T(8,128)(2,1)}, bf16[1728,288]{0,1:T(8,128)(2,1)}, u32[]{:S(2)}, u32[]{:S(2)}) collective-permute-start(bf16[1728,288]{0,1:T(8,128)(2,1)} %reshape.602), channel_id=1, source_target_pairs={{0,8},{4,12},{8,0},{12,4},{16,24},{20,28},{24,16},{28,20},{1,9},{5... | collective-permute-start | bytes 2985992 | tf_op jit(solution)/shard_map/ppermute | solution.py:82
  1004.6 77.6 %collective-permute-start.22 = (bf16[1152,1152]{1,0:T(8,128)(2,1)}, bf16[1152,1152]{1,0:T(8,128)(2,1)}, u32[]{:S(2)}, u32[]{:S(2)}) collective-permute-start(bf16[1152,1152]{1,0:T(8,128)(2,1)} %bitcast.340), channel_id=1, source_target_pairs={{0,2},{1,3},{2,0},{3,1},{4,6},{5,7},{6,4},{7,5},{8,10},{9,11},{10,... | collective-permute-start | bytes 7962632 | tf_op jit(solution)/shard_map/ppermute | solution.py:82
  1040.1 24.0 %collective-permute-start.9 = (bf16[864,288]{0,1:T(8,128)(2,1)}, bf16[864,288]{0,1:T(8,128)(2,1)}, u32[]{:S(2)}, u32[]{:S(2)}) collective-permute-start(bf16[864,288]{0,1:T(8,128)(2,1)} %bitcast.342), channel_id=1, source_target_pairs={{0,16},{4,20},{8,24},{12,28},{16,0},{20,4},{24,8},{28,12},{1,17},{... | collective-permute-start | bytes 1493000 | tf_op jit(solution)/shard_map/ppermute | solution.py:82
  1067.3 45.2 %collective-permute-start.10 = (bf16[432,288]{0,1:T(8,128)(2,1)S(1)}, bf16[432,288]{0,1:T(8,128)(2,1)}, u32[]{:S(2)}, u32[]{:S(2)}) collective-permute-start(bf16[432,288]{0,1:T(8,128)(2,1)S(1)} %bitcast.444), channel_id=1, source_target_pairs={{0,4},{4,0},{8,12},{12,8},{16,20},{20,16},{24,28},{28,24},{1,5},{5... | collective-permute-start | bytes 746504 | tf_op jit(solution)/shard_map/ppermute | solution.py:82
  1087.9 39.4 %collective-permute-start.23 = (bf16[576,1152]{1,0:T(8,128)(2,1)}, bf16[576,1152]{1,0:T(8,128)(2,1)}, u32[]{:S(2)}, u32[]{:S(2)}) collective-permute-start(bf16[576,1152]{1,0:T(8,128)(2,1)} %bitcast.78), channel_id=1, source_target_pairs={{0,8},{4,12},{8,0},{12,4},{16,24},{20,28},{24,16},{28,20},{1,9},{5... | collective-permute-start | bytes 3981320 | tf_op jit(solution)/shard_map/ppermute | solution.py:82
  1111.3 49.4 %collective-permute-start.18 = (bf16[288,2304]{1,0:T(8,128)(2,1)}, bf16[288,2304]{1,0:T(8,128)(2,1)}, u32[]{:S(2)}, u32[]{:S(2)}) collective-permute-start(bf16[288,2304]{1,0:T(8,128)(2,1)} %bitcast.142), channel_id=1, source_target_pairs={{0,8},{4,12},{8,0},{12,4},{16,24},{20,28},{24,16},{28,20},{1,9},{5... | collective-permute-start | bytes 3981320 | tf_op jit(solution)/shard_map/ppermute | solution.py:82
  1129.1 42.5 %collective-permute-start.24 = (bf16[288,1152]{1,0:T(8,128)(2,1)S(1)}, bf16[288,1152]{1,0:T(8,128)(2,1)}, u32[]{:S(2)}, u32[]{:S(2)}) collective-permute-start(bf16[288,1152]{1,0:T(8,128)(2,1)S(1)} %dynamic-slice_bitcast_fusion.2), channel_id=1, source_target_pairs={{0,16},{4,20},{8,24},{12,28},{16,0},{20,4},{24,8},{28,12},{1,17},{... | collective-permute-start | bytes 1990664 | tf_op jit(solution)/shard_map/ppermute | solution.py:82
  1169.4 29.8 %collective-permute-start.19 = (bf16[288,1152]{1,0:T(8,128)(2,1)S(1)}, bf16[288,1152]{1,0:T(8,128)(2,1)S(1)}, u32[]{:S(2)}, u32[]{:S(2)}) collective-permute-start(bf16[288,1152]{1,0:T(8,128)(2,1)S(1)} %bitcast.439), channel_id=1, source_target_pairs={{0,16},{4,20},{8,24},{12,28},{16,0},{20,4},{24,8},{28,12},{1,17},{... | collective-permute-start | bytes 1990664 | tf_op jit(solution)/shard_map/ppermute | solution.py:82
  1172.9 29.2 %collective-permute-start.25 = (bf16[144,1152]{1,0:T(8,128)(2,1)S(1)}, bf16[144,1152]{1,0:T(8,128)(2,1)S(1)}, u32[]{:S(2)}, u32[]{:S(2)}) collective-permute-start(bf16[144,1152]{1,0:T(8,128)(2,1)S(1)} %dynamic-slice_bitcast_fusion.4), channel_id=1, source_target_pairs={{0,4},{4,0},{8,12},{12,8},{16,20},{20,16},{24,28},{28,24},{1,5},{5... | collective-permute-start | bytes 995336 | tf_op jit(solution)/shard_map/ppermute | solution.py:82
  (92 other events, 1913.8 us)
Sparse Core Ops, SparseCore 0:
  9.6 58.5 all-gather.10
  69.7 25.7 all-gather.12
  97.0 70.9 all-gather.14
  169.4 70.9 all-gather.16
  742.6 58.4 all-gather.20
  889.6 71.8 all-gather.18

commit v2 on v1

--- a/solution.py
+++ b/solution.py
@@ -3,11 +3,16 @@
 import jax
 import jax.numpy as jnp
 from jax import lax
+from jax.experimental import pallas as pl
+from jax.experimental.pallas import tpu as pltpu
 from jax.sharding import PartitionSpec as P
 
 
 HIGHEST = lax.Precision.HIGHEST
 EVERY = ("seq", "mp")
+LANES = 128
+WINDOW = 256
+NT = (((1,), (1,)), ((), ()))
 
 
 def sinusoid(stamps, model_width):
@@ -31,50 +36,167 @@
     return inv * (kept - mean_kept - normal * mean_both)
 
 
-def split_heads(values, head_count):
-    row_count, model_width = values.shape
-    return values.reshape(row_count, head_count, model_width // head_count).transpose(1, 0, 2)
-
-
-def merge_heads(values):
-    head_count, row_count, head_size = values.shape
-    return values.transpose(1, 0, 2).reshape(row_count, head_count * head_size)
-
-
-def masked_scores(head_queries, head_keys, same_item, score_scale):
-    scores = (
-        jnp.einsum("qe,ke->qk", head_queries, head_keys, preferred_element_type=jnp.float32)
-        * score_scale
-    )
-    return jnp.where(same_item, scores, -1e30)
-
-
-def attend_forward(triple, same_item, score_scale):
-    head_queries, head_keys, head_values = triple
-    scores = masked_scores(head_queries, head_keys, same_item, score_scale)
-    row_max = jnp.max(scores, axis=1, keepdims=True)
-    exp_scores = jnp.exp(scores - row_max)
-    row_total = jnp.sum(exp_scores, axis=1, keepdims=True)
-    attention = (exp_scores / row_total).astype(jnp.bfloat16)
-    result = jnp.dot(attention, head_values, preferred_element_type=jnp.float32)
-    return (result, (row_max + jnp.log(row_total))[:, 0])
-
-
-def attend_backward(quintet, same_item, score_scale):
-    head_queries, head_keys, head_values, head_grad, log_total = quintet
-    scores = masked_scores(head_queries, head_keys, same_item, score_scale)
-    probs_full = jnp.exp(scores - log_total[:, None])
-    attention = probs_full.astype(jnp.bfloat16)
-    grad_soft = jnp.einsum("qe,ke->qk", head_grad, head_values, preferred_element_type=jnp.float32)
-    row_inner = jnp.sum(grad_soft * probs_full, axis=1, keepdims=True)
-    grad_scores = (probs_full * (grad_soft - row_inner)).astype(jnp.bfloat16)
-    grad_queries = jnp.dot(grad_scores, head_keys, preferred_element_type=jnp.float32) * score_scale
-    grad_keys = (
-        jnp.einsum("qk,qe->ke", grad_scores, head_queries, preferred_element_type=jnp.float32)
-        * score_scale
-    )
-    grad_values = jnp.einsum("qk,qe->ke", attention, head_grad, preferred_element_type=jnp.float32)
-    return (grad_queries, grad_keys, grad_values)
+def head_window(head_size, width):
+    first = pl.program_id(0) * head_size
+    tile = jnp.minimum(first // LANES, width // LANES - WINDOW // LANES)
+    start = first - tile * LANES
+    lane = lax.broadcasted_iota(jnp.int32, (1, WINDOW), 1)
+    inside = (lane >= start) & (lane < start + head_size)
+    return pl.multiple_of(tile * LANES, LANES), inside
+
+
+def dot32(left, right):
+    return jnp.dot(left, right, preferred_element_type=jnp.float32)
+
+
+def dot_nt(left, right):
+    return lax.dot_general(left, right, NT, preferred_element_type=jnp.float32)
+
+
+def attend_kernel(single_ref, gate_ref, q_ref, k_ref, v_ref, out_ref, log_ref, *, head_size, rows):
+    count, width = q_ref.shape
+    head = pl.program_id(0)
+    base, inside = head_window(head_size, width)
+    lanes = pl.ds(base, WINDOW)
+    scale = head_size ** (-0.5)
+    keys = k_ref[:, lanes] * inside.astype(jnp.bfloat16)
+    values_t = v_ref[:, lanes].T
+
+    def block(slot, first_key, key_count):
+        mine = slice(slot * rows, (slot + 1) * rows)
+        span = slice(first_key, first_key + key_count)
+        scores = dot_nt(keys[span], q_ref[mine, lanes])
+        peak = jnp.max(scores, axis=0, keepdims=True)
+        weights = jnp.exp((scores - peak) * scale)
+        total = jnp.sum(weights, axis=0, keepdims=True)
+        summed = dot32(values_t[:, span], weights.astype(jnp.bfloat16))
+        gate = gate_ref[slot, head].astype(jnp.float32)
+        result = (summed * (gate / total)).T.astype(jnp.bfloat16)
+        out_ref[mine, lanes] = jnp.where(inside, result, out_ref[mine, lanes])
+        log_ref[0, :, mine] = peak * scale + jnp.log(total)
+
+    @pl.when(single_ref[0] == 1)
+    def _():
+        for slot in range(count // rows):
+            block(slot, 0, count)
+
+    @pl.when(single_ref[0] == 0)
+    def _():
+        for slot in range(count // rows):
+            block(slot, slot * rows, rows)
+
+
+def attend_back_kernel(
+    single_ref,
+    gate_ref,
+    q_ref,
+    k_ref,
+    v_ref,
+    g_ref,
+    log_ref,
+    out_ref,
+    key_sum,
+    value_sum,
+    *,
+    head_size,
+    rows,
+):
+    count, width = q_ref.shape
+    head = pl.program_id(0)
+    base, inside = head_window(head_size, width)
+    lanes = pl.ds(base, WINDOW)
+    scale = head_size ** (-0.5)
+    only = inside.astype(jnp.bfloat16)
+    keys = k_ref[:, lanes] * only
+    keys_t = keys.T
+    values = v_ref[:, lanes]
+
+    def put(part, mine, result):
+        there = pl.ds(pl.multiple_of(base + part * width, LANES), WINDOW)
+        out_ref[mine, there] = jnp.where(
+            inside, result.astype(jnp.bfloat16), out_ref[mine, there]
+        )
+
+    def block(slot, first_key, key_count):
+        mine = slice(slot * rows, (slot + 1) * rows)
+        span = slice(first_key, first_key + key_count)
+        queries = q_ref[mine, lanes]
+        gate = gate_ref[slot, head].astype(jnp.float32)
+        grads = g_ref[mine, lanes] * (only.astype(jnp.float32) * gate).astype(jnp.bfloat16)
+        scores = dot_nt(keys[span], queries)
+        probs = jnp.exp(scores * scale - log_ref[0, :, mine])
+        soft = dot_nt(values[span], grads)
+        inner = jnp.sum(soft * probs, axis=0, keepdims=True)
+        grad_scores = (probs * (soft - inner)).astype(jnp.bfloat16)
+        put(0, mine, (dot32(keys_t[:, span], grad_scores) * scale).T)
+        return dot32(grad_scores, queries), dot32(probs.astype(jnp.bfloat16), grads)
+
+    @pl.when(single_ref[0] == 1)
+    def _():
+        for slot in range(count // rows):
+            key_part, value_part = block(slot, 0, count)
+            if slot == 0:
+                key_sum[...] = key_part
+                value_sum[...] = value_part
+            else:
+                key_sum[...] += key_part
+                value_sum[...] += value_part
+        put(1, slice(None), key_sum[...] * scale)
+        put(2, slice(None), value_sum[...])
+
+    @pl.when(single_ref[0] == 0)
+    def _():
+        for slot in range(count // rows):
+            mine = slice(slot * rows, (slot + 1) * rows)
+            key_part, value_part = block(slot, slot * rows, rows)
+            put(1, mine, key_part * scale)
+            put(2, mine, value_part)
+
+
+def whole(shape):
+    return pl.BlockSpec(shape, lambda n, *_: (0,) * len(shape))
+
+
+def attend(single, gates, queries, keys, values):
+    count, width = queries.shape
+    heads = gates.shape[1]
+    log_spec = pl.BlockSpec((1, 1, count), lambda n, *_: (n, 0, 0))
+    return pl.pallas_call(
+        lambda *refs: attend_kernel(
+            *refs, head_size=width // heads, rows=count // gates.shape[0]
+        ),
+        grid_spec=pltpu.PrefetchScalarGridSpec(
+            num_scalar_prefetch=2,
+            grid=(heads,),
+            in_specs=[whole((count, width))] * 3,
+            out_specs=[whole((count, width)), log_spec],
+        ),
+        out_shape=[
+            jax.ShapeDtypeStruct((count, width), jnp.bfloat16),
+            jax.ShapeDtypeStruct((heads, 1, count), jnp.float32),
+        ],
+        name="attend",
+    )(single, gates, queries, keys, values)
+
+
+def attend_back(single, gates, queries, keys, values, grads, logs):
+    count, width = queries.shape
+    heads = gates.shape[1]
+    log_spec = pl.BlockSpec((1, 1, count), lambda n, *_: (n, 0, 0))
+    return pl.pallas_call(
+        lambda *refs: attend_back_kernel(
+            *refs, head_size=width // heads, rows=count // gates.shape[0]
+        ),
+        grid_spec=pltpu.PrefetchScalarGridSpec(
+            num_scalar_prefetch=2,
+            grid=(heads,),
+            in_specs=[whole((count, width))] * 4 + [log_spec],
+            out_specs=whole((count, 3 * width)),
+            scratch_shapes=[pltpu.VMEM((count, WINDOW), jnp.float32)] * 2,
+        ),
+        out_shape=jax.ShapeDtypeStruct((count, 3 * width), jnp.bfloat16),
+        name="attend_back",
+    )(single, gates, queries, keys, values, grads, logs)
 
 
 def swap(values, axis_name, bit):
@@ -161,10 +283,8 @@
 ):
     row_count, model_width = tokens.shape
     slot_count = timestep.shape[0]
-    head_count = head_mask.shape[1]
     group_count = chan_mask.shape[1]
     hidden_width = up_bias.shape[0]
-    score_scale = (model_width // head_count) ** (-0.5)
     mp_size = lax.axis_size("mp")
     seq_size = lax.axis_size("seq")
     slot_rows = row_count // slot_count
@@ -198,8 +318,6 @@
         slot_mod[:, None, section * model_width : (section + 1) * model_width]
         for section in range(6)
     ]
-    head_gate = jnp.where(single, head_mask[:1], head_mask).astype(jnp.float32)
-    head_rows = jnp.repeat(head_gate, slot_rows, axis=0)
     chan_gate = jnp.where(single, chan_mask[:1], chan_mask).astype(jnp.float32)
     unit_gate = jnp.repeat(chan_gate, hidden_width // group_count, axis=1)[:, None, :]
     keep_rows = router_keep.astype(jnp.float32).reshape(slot_count, slot_rows, 1)
@@ -212,16 +330,9 @@
     queries = (joined[:, :model_width] + qv_float[:model_width]).astype(jnp.bfloat16)
     keys_all = joined[:, model_width : 2 * model_width].astype(jnp.bfloat16)
     values_all = (joined[:, 2 * model_width :] + qv_float[model_width:]).astype(jnp.bfloat16)
-    same_item = segment[:, None] == segment[None, :]
-    head_inputs = (
-        split_heads(queries, head_count),
-        split_heads(keys_all, head_count),
-        split_heads(values_all, head_count),
-    )
-    attended, log_total = lax.map(
-        lambda triple: attend_forward(triple, same_item, score_scale), head_inputs
-    )
-    attn_cat = merge_heads(attended * head_rows.T[:, :, None]).astype(jnp.bfloat16)
+    lone_flag = single.astype(jnp.int32).reshape(1)
+    gates = jnp.where(single, head_mask[:1], head_mask)
+    attn_cat, log_total = attend(lone_flag, gates, queries, keys_all, values_all)
     branch = jnp.dot(attn_cat, full_proj, preferred_element_type=jnp.float32) + proj_bias.astype(
         jnp.float32
     )
@@ -295,14 +406,9 @@
         axis=0,
     )
     all_early = lax.all_gather(early_rows, EVERY, axis=0, tiled=False)
-    grad_heads = split_heads(grad_cat, head_count) * head_rows.T[:, :, None].astype(jnp.bfloat16)
-    grad_queries, grad_keys, grad_values = lax.map(
-        lambda quintet: attend_backward(quintet, same_item, score_scale),
-        head_inputs + (grad_heads, log_total),
-    )
-    grad_joined = jnp.concatenate(
-        [merge_heads(grad_queries), merge_heads(grad_keys), merge_heads(grad_values)], axis=1
-    ).astype(jnp.bfloat16)
+    grad_joined = attend_back(
+        lone_flag, gates, queries, keys_all, values_all, grad_cat, log_total
+    )
     grad_normed = jnp.einsum("ne,de->nd", grad_joined, full_qkv, preferred_element_type=jnp.float32)
     qkv_piece = grad_sum(normed, grad_joined, False)
     column_sums = jnp.sum(grad_joined.astype(jnp.float32), axis=0)

time: 1230 us -> 1010 us (0.82)
  matrix products: 460 us -> 205 us
  Pallas kernels: 0 us -> 141 us
  local copies, waits for them, and re-layouts: 393 us -> 324 us
  other arithmetic: 179 us -> 136 us
    dot_general x112 -> x0, matrix products: 248 us -> none  [the longest x32 61.7 us: masked_scores(): jnp.einsum('qe,ke->qk', head_queries, head_keys, preferred_element_type=j...]
    pallas_call x0 -> x2, Pallas kernels: none -> 141 us  [the longest x1 86.6 us: attend_back(): pl.pallas_call(lambda *refs: attend_back_kernel(*refs, head_size=width //...]
    unnamed x183 -> x161, local copies, waits for them, and re-layouts: 43 us -> 18.9 us
    convert_element_type x18 -> x0, other arithmetic: 23.2 us -> none  [the longest x16 18.2 us: attend_backward(): grad_scores = (probs_full * (grad_soft - row_inner)).astype(jnp.bfloat16)]
    dynamic_update_slice x16 -> x0, local copies, waits for them, and re-layouts: 22.3 us -> none  [on_device(): lax.map(lambda triple: attend_forward(triple, same_item, score_scale), he...]
    reduce_sum x16 -> x0, other arithmetic: 16.4 us -> none  [attend_forward(): row_total = jnp.sum(exp_scores, axis=1, keepdims=True)]
    dynamic_slice x11 -> x10, local copies, waits for them, and re-layouts: 57 us -> 56.9 us  [pick(): cut = lax.dynamic_index_in_dim(cut, index, dim + 1, keepdims=False)]
  transfers between devices with their start and end apart: 32 -> 32, of which waited for: 11 -> 11; matrix products, arithmetic and copies ran while one was open for 58% -> 55% of each run, Pallas kernels for 0% -> 5%
where the time goes in v2:
time: 1010 us; the launch traced here: 998 us
  local copies, waits for them, and re-layouts  324 us (32%)
  matrix products  205 us (20%)
  waiting for transfers between devices  152 us (15%)
  Pallas kernels  141 us (14%)
  other arithmetic  136 us (13%)
  starting transfers between devices  23 us (2%)
  between operations  16.4 us (2%)
    ppermute x26, waiting for transfers between devices, swap(): return lax.ppermute(values, axis_name, [(i, i ^ bit) for i in range(size)])  149 us
    pallas_call x1, Pallas kernels, attend_back(): pl.pallas_call(lambda *refs: attend_back_kernel(*refs, head_size=width //...  86.6 us
    mul x4, local copies, waits for them, and re-layouts, on_device(): value * unit_gate  59.3 us
    dynamic_slice x10, local copies, waits for them, and re-layouts, pick(): cut = lax.dynamic_index_in_dim(cut, index, dim + 1, keepdims=False)  56.9 us
    pallas_call x1, Pallas kernels, attend(): pl.pallas_call(lambda *refs: attend_kernel(*refs, head_size=width // head...  54.6 us
    reshape x2, local copies, waits for them, and re-layouts, on_device(): pre_act.reshape(slot_count, slot_rows, hidden_width)  50.3 us
    dot_general x6, matrix products, product(): jnp.einsum('ne,nd->ed', whole_side, side, preferred_element_type=jnp.floa...  42.1 us
    reshape x9, local copies, waits for them, and re-layouts, pick(): cut = values.reshape(shape[:dim] + (major, 2, inner) + shape[dim + 1:])  33.9 us
  transfers between devices with their start and end apart: 32, of which 11 were waited for; matrix products, arithmetic and copies ran while one was open for 55% of the time, Pallas kernels for 5%

profile of v2, /device:TPU:0, one launch (start us, length us, event | category | flops | bytes accessed | tf_op | source)
XLA Modules:
  0.0 997.9 jit_solution(10845691070505007748)
XLA Ops:
  32.2 22.0 %mul.490 = f32[1024,2,2,1152]{3,2,1,0:T(2,128)} reshape(f32[4,256,4608]{2,1,0:T(8,128)} %mul.420) | data formatting | bytes 37748736 | tf_op jit(solution)/shard_map/mul | solution.py:349
  54.3 28.3 %copy.226 = f32[1024,2,2,1152]{0,3,1,2:T(8,128)} copy(f32[1024,2,2,1152]{3,2,1,0:T(2,128)} %mul.490) | data formatting | bytes 37748736 | tf_op jit(solution)/shard_map/mul | solution.py:349
  166.8 13.0 %fusion.60 = f32[1024,3456]{1,0:T(8,128)S(1)} fusion(bf16[1024,1152]{1,0:T(8,128)(2,1)} %fusion.7, bf16[1152,3456]{1,0:T(8,128)(2,1)} %all-gather.11.cloned.1.call-done), kind=kOutput, calls=%fused_computation.206 | convolution fusion | flops 8153726976 | bytes 24477696 | tf_op jit(solution)/shard_map/dot_general | solution.py:328
  184.8 54.6 %attend.1 = (bf16[1024,1152]{1,0:T(8,128)(2,1)}, f32[16,1,1024]{2,1,0:T(1,128)}) custom-call(s32[1]{0:T(128)S(6)} %reshape.523.refs_0_, s32[4,16]{1,0:T(4,128)} %broadcast_select_fusion.1.refs_1_, bf16[1024,1152]{1,0:T(8,128)(2,1)} %get-tuple-element.38.refs_2_, bf16[1024,1152]{1,0:T(8,128)(2,1)} %slice.172.refs_3_, bf16[1024,1152]{1,0:T(8,128)(2,1)} %get-tuple-element.37.refs_4_), custom_call_target="tpu_custom_call" | custom-call | tf_op jit(solution)/shard_map/attend/pallas_call | solution.py:164
  265.9 11.6 %add_convert_fusion.3 = (bf16[1024,2,2,288]{0,3,2,1:T(8,128)(2,1)S(1)}, bf16[1024,2,2,288]{0,3,2,1:T(8,128)(2,1)S(1)}) fusion(f32[1024,2,2,288]{0,3,2,1:T(8,128)} %add.396, f32[1024,2,2,288]{0,3,2,1:T(8,128)} %mul.481, f32[1024,2,2,288]{0,3,2,1:T(8,128)} %bitcast.262, f32[1024,2,2,288]{0,3,2,1:T(8,128)} %mul.477, f32[1024,2,2,288]{0,3,2,1:T(8,128)S(1)} %bitcast.263, ...), kind=kLoop, calls=%fused_computation.48 | loop fusion | flops 14155776 | bytes 37765120 | tf_op jit(solution)/shard_map/convert_element_type | solution.py:342
  279.4 23.3 %fusion = (bf16[1024,4608]{1,0:T(8,128)(2,1)}, f32[1024,4608]{1,0:T(8,128)}) fusion(f32[4,4608]{1,0:T(4,128)} %copy-done.24, f32[4608]{0:T(1024)} %convert_element_type.347, bf16[1024,1152]{1,0:T(8,128)(2,1)S(1)} %fusion.9, bf16[1152,4608]{1,0:T(8,128)(2,1)} %all-gather.15.cloned.1.call-done), kind=kOutput, calls=%fused_computation.1 | convolution fusion | flops 10923540480 | bytes 41379840 | tf_op jit(solution)/shard_map/dot_general | solution.py:345
  302.7 22.2 %reshape.566 = f32[1024,2,2,1152]{3,2,1,0:T(2,128)} reshape(f32[1024,4608]{1,0:T(8,128)} %get-tuple-element.84) | data formatting | bytes 37748736 | tf_op jit(solution)/shard_map/reshape | solution.py:348
  324.9 27.1 %convert_reduce_fusion = (f32[4608]{0:T(1024)}, bf16[4,256,4608]{2,1,0:T(8,128)(2,1)}) fusion(f32[4,256,4608]{2,1,0:T(8,128)} %bitcast.259, f32[4,4608]{1,0:T(4,128)} %copy-done.24, bf16[4,256,1152]{2,1,0:T(8,128)(2,1)S(1)} %bitcast.283, bf16[4608,1152]{1,0:T(8,128)(2,1)} %all-gather.17.cloned.1.call-done), kind=kOutput, calls=%fused_computation.3 | convolution fusion | flops 10970722304 | bytes 41379840 | tf_op jit(solution)/shard_map/nd,fd->nf/dot_general | solution.py:360
  352.0 20.7 %fusion.20 = (f32[1024]{0:T(1024)}, f32[1024]{0:T(1024)}, bf16[1024,1152]{1,0:T(8,128)(2,1)}) fusion(f32[4,1152]{1,0:T(4,128)} %get-tuple-element.69, f32[1024]{0:T(1024)S(1)} %add_rsqrt_fusion, f32[1024,1152]{1,0:T(8,128)} %copy-done.2, f32[1024]{0:T(1024)S(1)} %broadcast_multiply_fusion.4, bf16[1024,4608]{1,0:T(8,128)(2,1)} %bitcast.299, ...), kind=kOutput, calls=%fused_computation.66 | convolution fusion | flops 10881071104 | bytes 27166720 | tf_op jit(solution)/shard_map/nf,df->nd/dot_general | solution.py:367
  376.6 24.7 %convert_reduce_fusion.2 = (f32[1152]{0:T(1024)}, bf16[1024,1152]{1,0:T(8,128)(2,1)}, f32[1024,1152]{1,0:T(8,128)}, bf16[1024,1152]{1,0:T(8,128)(2,1)}, f32[1024,1152]{1,0:T(8,128)}) fusion(f32[4,1152]{1,0:T(4,128)} %get-tuple-element.72, f32[1024]{0:T(1024)} %get-tuple-element.89, f32[1024,1152]{1,0:T(8,128)} %copy-done.2, ...), kind=kOutput, calls=%fused_computation.50 | convolution fusion | flops 10896407552 | bytes 43731968 | tf_op jit(solution)/shard_map/dot_general | solution.py:351
  408.1 86.6 %attend_back.1 = bf16[1024,3456]{1,0:T(8,128)(2,1)} custom-call(s32[1]{0:T(128)S(6)} %reshape.523.refs_0_, s32[4,16]{1,0:T(4,128)} %broadcast_select_fusion.1.refs_1_, bf16[1024,1152]{1,0:T(8,128)(2,1)} %get-tuple-element.38.refs_2_, bf16[1024,1152]{1,0:T(8,128)(2,1)} %slice.172.refs_3_, bf16[1024,1152]{1,0:T(8,128)(2,1)} %get-tuple-element.37.refs_4_, ...), custom_call_target="tpu_custom_call" | custom-call | tf_op jit(solution)/shard_map/attend_back/pallas_call | solution.py:186
  499.1 15.4 %fusion.19 = (f32[1024]{0:T(1024)}, f32[1024]{0:T(1024)}, f32[1024,1152]{1,0:T(8,128)S(1)}) fusion(f32[4,1152]{1,0:T(4,128)S(1)} %copy-done.30, f32[1024]{0:T(1024)S(1)} %add_rsqrt_fusion.1, f32[1024]{0:T(1024)S(1)} %broadcast_multiply_fusion.5, bf16[1024,1152]{1,0:T(8,128)(2,1)S(1)} %copy-done.1, bf16[1024,3456]{1,0:T(8,128)(2,1)} %attend_back.1, ...), kind=kOutput, calls=%fused_computation.65 | convolution fusion | flops 8161982464 | bytes 22153216 | tf_op jit(solution)/shard_map/ne,de->nd/dot_general | solution.py:412
  545.0 28.2 %copy.221 = f32[1024,2,2,1152]{0,3,1,2:T(8,128)} copy(f32[1024,2,2,1152]{3,2,1,0:T(2,128)} %reshape.566) | data formatting | bytes 37748736 | tf_op jit(solution)/shard_map/reshape | solution.py:348
  573.1 17.9 %multiply_convert_fusion = bf16[1024,2,2,1152]{0,3,1,2:T(8,128)(2,1)} fusion(f32[1024,2,2,1152]{0,3,1,2:T(8,128)} %copy.226, f32[1024,2,2,1152]{0,3,1,2:T(8,128)} %copy.221), kind=kLoop, calls=%fused_computation.2 | loop fusion | flops 47185920 | bytes 47185920 | tf_op jit(solution)/shard_map/convert_element_type | solution.py:349
  613.6 15.7 %collective-permute-done.12 = bf16[1152,288]{0,1:T(8,128)(2,1)} collective-permute-done((bf16[1152,288]{0,1:T(8,128)(2,1)S(1)}, bf16[1152,288]{0,1:T(8,128)(2,1)}, u32[]{:S(2)}, u32[]{:S(2)}) %collective-permute-start.12) | collective-permute-done | bytes 663584 | tf_op jit(solution)/shard_map/ppermute | solution.py:204
  692.3 10.7 %add_convert_fusion.1 = bf16[576,4608]{1,0:T(8,128)(2,1)S(1)} fusion(bf16[576,4608]{1,0:T(8,128)(2,1)} %collective-permute-done.16, bf16[1024,576]{0,1:T(8,128)(2,1)S(1)} %bitcast.288, bf16[1024,4608]{1,0:T(8,128)(2,1)} %bitcast.300), kind=kOutput, calls=%fused_computation.10 | convolution fusion | flops 5443780608 | bytes 21233664 | tf_op jit(solution)/shard_map/nd,ne->de/dot_general | solution.py:237
  717.2 11.0 %reshape.569 = bf16[1152,1,2,1152]{3,2,0,1:T(2,128)(2,1)} reshape(bf16[1152,2304]{1,0:T(8,128)(2,1)} %add_convert_fusion) | data formatting | bytes 10616832 | tf_op jit(solution)/shard_map/reshape | solution.py:210
  728.2 18.9 %collective-permute-done.7 = bf16[3456,288]{0,1:T(8,128)(2,1)S(1)} collective-permute-done((bf16[3456,288]{0,1:T(8,128)(2,1)}, bf16[3456,288]{0,1:T(8,128)(2,1)S(1)}, u32[]{:S(2)}, u32[]{:S(2)}) %collective-permute-start.7) | collective-permute-done | bytes 1990688 | tf_op jit(solution)/shard_map/ppermute | solution.py:204
  765.7 13.7 %constant_dynamic-slice_fusion.3 = (bf16[1152,1,1,1152]{3,2,0,1:T(2,128)(2,1)}, bf16[1152,1,1,1152]{3,2,0,1:T(2,128)(2,1)S(1)}) fusion(bf16[1152,1,2,1152]{3,2,0,1:T(2,128)(2,1)} %reshape.569, s32[]{:T(128)S(6)} %select_n.144, s32[]{:T(128)S(6)} %select_n.145), kind=kLoop, calls=%fused_computation.162 | loop fusion | bytes 10616840 | tf_op jit(solution)/shard_map/jit(dynamic_index_in_dim)/dynamic_slice | solution.py:211
  830.4 10.9 %collective-permute-done.9 = bf16[864,288]{0,1:T(8,128)(2,1)} collective-permute-done((bf16[864,288]{0,1:T(8,128)(2,1)}, bf16[864,288]{0,1:T(8,128)(2,1)}, u32[]{:S(2)}, u32[]{:S(2)}) %collective-permute-start.9) | collective-permute-done | bytes 497696 | tf_op jit(solution)/shard_map/ppermute | solution.py:204
  845.0 14.9 %collective-permute-done.22 = bf16[1152,1152]{1,0:T(8,128)(2,1)} collective-permute-done((bf16[1152,1152]{1,0:T(8,128)(2,1)}, bf16[1152,1152]{1,0:T(8,128)(2,1)}, u32[]{:S(2)}, u32[]{:S(2)}) %collective-permute-start.22) | collective-permute-done | bytes 2654240 | tf_op jit(solution)/shard_map/ppermute | solution.py:204
  891.8 10.9 %convert_reduce_fusion.5 = f32[288,2,1152]{2,1,0:T(2,128)} fusion(bf16[288,2,2,1152]{3,2,1,0:T(2,128)(2,1)S(1)} %reshape.560, s32[]{:T(128)S(6)} %select_n.146), kind=kLoop, calls=%fused_computation.79 | loop fusion | flops 663552 | bytes 3981316 | tf_op jit(solution)/shard_map/convert_element_type | solution.py:222
  907.8 30.9 %collective-permute-done.18 = bf16[288,2304]{1,0:T(8,128)(2,1)} collective-permute-done((bf16[288,2304]{1,0:T(8,128)(2,1)}, bf16[288,2304]{1,0:T(8,128)(2,1)}, u32[]{:S(2)}, u32[]{:S(2)}) %collective-permute-start.18) | collective-permute-done | bytes 1327136 | tf_op jit(solution)/shard_map/ppermute | solution.py:204
  949.7 27.1 %collective-permute-done.19 = bf16[288,1152]{1,0:T(8,128)(2,1)S(1)} collective-permute-done((bf16[288,1152]{1,0:T(8,128)(2,1)S(1)}, bf16[288,1152]{1,0:T(8,128)(2,1)S(1)}, u32[]{:S(2)}, u32[]{:S(2)}) %collective-permute-start.19) | collective-permute-done | bytes 663584 | tf_op jit(solution)/shard_map/ppermute | solution.py:204
  (377 shorter events, 421.1 us)
Async XLA Ops:
  7.3 159.6 %all-gather.11.cloned.1.call-start = ((), (), s32[]{:S(2)}) async-start(), calls=%async_computation | async-start | bytes 9953280 | tf_op jit(solution)/shard_map/all_gather | solution.py:311
  8.0 231.5 %all-gather.13.cloned.1.call-start = ((), (), s32[]{:S(2)}) async-start(), calls=%async_computation.1 | async-start | bytes 3317760 | tf_op jit(solution)/shard_map/all_gather | solution.py:312
  8.7 270.6 %all-gather.15.cloned.1.call-start = ((), (), s32[]{:S(2)}) async-start(), calls=%async_computation.2 | async-start | bytes 13271040 | tf_op jit(solution)/shard_map/all_gather | solution.py:313
  9.5 315.4 %all-gather.17.cloned.1.call-start = ((), (), s32[]{:S(2)}) async-start(), calls=%async_computation.3 | async-start | bytes 13271040 | tf_op jit(solution)/shard_map/all_gather | solution.py:314
  10.1 665.0 %all-gather.21.cloned.1.call-start = ((), (), s32[]{:S(2)}) async-start(), calls=%async_computation.5 | async-start | bytes 2433024 | tf_op jit(solution)/shard_map/all_gather | solution.py:424
  10.1 73.7 %collective-permute-start.2 = (f32[4]{0:T(128)S(1)}, f32[4]{0:T(128)S(1)}, u32[]{:S(2)}, u32[]{:S(2)}) collective-permute-start(f32[4]{0:T(128)S(1)} %convert_element_type.336), channel_id=1, source_target_pairs={{0,3},{1,2},{2,1},{3,0},{4,7},{5,6},{6,5},{7,4},{8,11},{9,10},{10,... | collective-permute-start | bytes 56 | tf_op jit(solution)/shard_map/ppermute | solution.py:204
  12.6 71.2 %collective-permute-start.1 = (f32[4]{0:T(128)S(1)}, f32[4]{0:T(128)S(1)}, u32[]{:S(2)}, u32[]{:S(2)}) collective-permute-start(f32[4]{0:T(128)S(1)} %convert_element_type.336), channel_id=1, source_target_pairs={{0,2},{1,3},{2,0},{3,1},{4,6},{5,7},{6,4},{7,5},{8,10},{9,11},{10,... | collective-permute-start | bytes 56 | tf_op jit(solution)/shard_map/ppermute | solution.py:204
  13.3 70.6 %collective-permute-start = (f32[4]{0:T(128)S(1)}, f32[4]{0:T(128)S(1)}, u32[]{:S(2)}, u32[]{:S(2)}) collective-permute-start(f32[4]{0:T(128)S(1)} %convert_element_type.336), channel_id=1, source_target_pairs={{0,1},{1,0},{2,3},{3,2},{4,5},{5,4},{6,7},{7,6},{8,9},{9,8},{10,11... | collective-permute-start | bytes 56 | tf_op jit(solution)/shard_map/ppermute | solution.py:204
  524.9 270.5 %all-gather.19.cloned.1.call-start = ((), (), s32[]{:S(2)}) async-start(), calls=%async_computation.4 | async-start | bytes 4866048 | tf_op jit(solution)/shard_map/all_gather | solution.py:408
  534.2 146.3 %collective-permute-start.6 = (bf16[3456,576]{0,1:T(8,128)(2,1)}, bf16[3456,576]{0,1:T(8,128)(2,1)}, u32[]{:S(2)}, u32[]{:S(2)}) collective-permute-start(bf16[3456,576]{0,1:T(8,128)(2,1)} %convolution_convert_fusion.2), channel_id=1, source_target_pairs={{0,1},{1,0},{2,3},{3,2},{4,5},{5,4},{6,7},{7,6},{8,9},{9,8},{10,11... | collective-permute-start | bytes 11943944 | tf_op jit(solution)/shard_map/ppermute | solution.py:204
  537.0 70.6 %collective-permute-start.11 = (bf16[1152,576]{0,1:T(8,128)(2,1)}, bf16[1152,576]{0,1:T(8,128)(2,1)}, u32[]{:S(2)}, u32[]{:S(2)}) collective-permute-start(bf16[1152,576]{0,1:T(8,128)(2,1)} %convolution_convert_fusion.5), channel_id=1, source_target_pairs={{0,1},{1,0},{2,3},{3,2},{4,5},{5,4},{6,7},{7,6},{8,9},{9,8},{10,11... | collective-permute-start | bytes 3981320 | tf_op jit(solution)/shard_map/ppermute | solution.py:204
  544.9 146.2 %collective-permute-start.16 = (bf16[576,4608]{1,0:T(8,128)(2,1)}, bf16[576,4608]{1,0:T(8,128)(2,1)}, u32[]{:S(2)}, u32[]{:S(2)}) collective-permute-start(bf16[576,4608]{1,0:T(8,128)(2,1)} %convolution_convert_fusion.1), channel_id=1, source_target_pairs={{0,1},{1,0},{2,3},{3,2},{4,5},{5,4},{6,7},{7,6},{8,9},{9,8},{10,11... | collective-permute-start | bytes 15925256 | tf_op jit(solution)/shard_map/ppermute | solution.py:204
  613.6 94.5 %collective-permute-start.21 = (bf16[1152,2304]{1,0:T(8,128)(2,1)}, bf16[1152,2304]{1,0:T(8,128)(2,1)}, u32[]{:S(2)}, u32[]{:S(2)}) collective-permute-start(bf16[1152,2304]{1,0:T(8,128)(2,1)} %convolution_convert_fusion), channel_id=1, source_target_pairs={{0,1},{1,0},{2,3},{3,2},{4,5},{5,4},{6,7},{7,6},{8,9},{9,8},{10,11... | collective-permute-start | bytes 15925256 | tf_op jit(solution)/shard_map/ppermute | solution.py:204
  690.7 56.4 %collective-permute-start.7 = (bf16[3456,288]{0,1:T(8,128)(2,1)}, bf16[3456,288]{0,1:T(8,128)(2,1)S(1)}, u32[]{:S(2)}, u32[]{:S(2)}) collective-permute-start(bf16[3456,288]{0,1:T(8,128)(2,1)} %dynamic-slice_bitcast_fusion.1), channel_id=1, source_target_pairs={{0,2},{1,3},{2,0},{3,1},{4,6},{5,7},{6,4},{7,5},{8,10},{9,11},{10,... | collective-permute-start | bytes 5971976 | tf_op jit(solution)/shard_map/ppermute | solution.py:204
  707.5 158.1 %collective-permute-start.17 = (bf16[288,4608]{1,0:T(8,128)(2,1)}, bf16[288,4608]{1,0:T(8,128)(2,1)}, u32[]{:S(2)}, u32[]{:S(2)}) collective-permute-start(bf16[288,4608]{1,0:T(8,128)(2,1)} %dynamic-slice_bitcast_fusion), channel_id=1, source_target_pairs={{0,2},{1,3},{2,0},{3,1},{4,6},{5,7},{6,4},{7,5},{8,10},{9,11},{10,... | collective-permute-start | bytes 7962632 | tf_op jit(solution)/shard_map/ppermute | solution.py:204
  765.5 40.2 %collective-permute-start.8 = (bf16[1728,288]{0,1:T(8,128)(2,1)}, bf16[1728,288]{0,1:T(8,128)(2,1)}, u32[]{:S(2)}, u32[]{:S(2)}) collective-permute-start(bf16[1728,288]{0,1:T(8,128)(2,1)} %reshape.539), channel_id=1, source_target_pairs={{0,8},{4,12},{8,0},{12,4},{16,24},{20,28},{24,16},{28,20},{1,9},{5... | collective-permute-start | bytes 2985992 | tf_op jit(solution)/shard_map/ppermute | solution.py:204
  781.4 78.5 %collective-permute-start.22 = (bf16[1152,1152]{1,0:T(8,128)(2,1)}, bf16[1152,1152]{1,0:T(8,128)(2,1)}, u32[]{:S(2)}, u32[]{:S(2)}) collective-permute-start(bf16[1152,1152]{1,0:T(8,128)(2,1)} %bitcast.254), channel_id=1, source_target_pairs={{0,2},{1,3},{2,0},{3,1},{4,6},{5,7},{6,4},{7,5},{8,10},{9,11},{10,... | collective-permute-start | bytes 7962632 | tf_op jit(solution)/shard_map/ppermute | solution.py:204
  817.3 24.0 %collective-permute-start.9 = (bf16[864,288]{0,1:T(8,128)(2,1)}, bf16[864,288]{0,1:T(8,128)(2,1)}, u32[]{:S(2)}, u32[]{:S(2)}) collective-permute-start(bf16[864,288]{0,1:T(8,128)(2,1)} %bitcast.256), channel_id=1, source_target_pairs={{0,16},{4,20},{8,24},{12,28},{16,0},{20,4},{24,8},{28,12},{1,17},{... | collective-permute-start | bytes 1493000 | tf_op jit(solution)/shard_map/ppermute | solution.py:204
  844.5 45.4 %collective-permute-start.10 = (bf16[432,288]{0,1:T(8,128)(2,1)S(1)}, bf16[432,288]{0,1:T(8,128)(2,1)}, u32[]{:S(2)}, u32[]{:S(2)}) collective-permute-start(bf16[432,288]{0,1:T(8,128)(2,1)S(1)} %bitcast.298), channel_id=1, source_target_pairs={{0,4},{4,0},{8,12},{12,8},{16,20},{20,16},{24,28},{28,24},{1,5},{5... | collective-permute-start | bytes 746504 | tf_op jit(solution)/shard_map/ppermute | solution.py:204
  865.6 39.2 %collective-permute-start.23 = (bf16[576,1152]{1,0:T(8,128)(2,1)}, bf16[576,1152]{1,0:T(8,128)(2,1)}, u32[]{:S(2)}, u32[]{:S(2)}) collective-permute-start(bf16[576,1152]{1,0:T(8,128)(2,1)} %bitcast.57), channel_id=1, source_target_pairs={{0,8},{4,12},{8,0},{12,4},{16,24},{20,28},{24,16},{28,20},{1,9},{5... | collective-permute-start | bytes 3981320 | tf_op jit(solution)/shard_map/ppermute | solution.py:204
  887.9 50.8 %collective-permute-start.18 = (bf16[288,2304]{1,0:T(8,128)(2,1)}, bf16[288,2304]{1,0:T(8,128)(2,1)}, u32[]{:S(2)}, u32[]{:S(2)}) collective-permute-start(bf16[288,2304]{1,0:T(8,128)(2,1)} %bitcast.97), channel_id=1, source_target_pairs={{0,8},{4,12},{8,0},{12,4},{16,24},{20,28},{24,16},{28,20},{1,9},{5... | collective-permute-start | bytes 3981320 | tf_op jit(solution)/shard_map/ppermute | solution.py:204
  906.5 41.3 %collective-permute-start.24 = (bf16[288,1152]{1,0:T(8,128)(2,1)S(1)}, bf16[288,1152]{1,0:T(8,128)(2,1)}, u32[]{:S(2)}, u32[]{:S(2)}) collective-permute-start(bf16[288,1152]{1,0:T(8,128)(2,1)S(1)} %dynamic-slice_bitcast_fusion.2), channel_id=1, source_target_pairs={{0,16},{4,20},{8,24},{12,28},{16,0},{20,4},{24,8},{28,12},{1,17},{... | collective-permute-start | bytes 1990664 | tf_op jit(solution)/shard_map/ppermute | solution.py:204
  947.5 29.3 %collective-permute-start.19 = (bf16[288,1152]{1,0:T(8,128)(2,1)S(1)}, bf16[288,1152]{1,0:T(8,128)(2,1)S(1)}, u32[]{:S(2)}, u32[]{:S(2)}) collective-permute-start(bf16[288,1152]{1,0:T(8,128)(2,1)S(1)} %bitcast.296), channel_id=1, source_target_pairs={{0,16},{4,20},{8,24},{12,28},{16,0},{20,4},{24,8},{28,12},{1,17},{... | collective-permute-start | bytes 1990664 | tf_op jit(solution)/shard_map/ppermute | solution.py:204
  949.2 30.5 %collective-permute-start.25 = (bf16[144,1152]{1,0:T(8,128)(2,1)S(1)}, bf16[144,1152]{1,0:T(8,128)(2,1)S(1)}, u32[]{:S(2)}, u32[]{:S(2)}) collective-permute-start(bf16[144,1152]{1,0:T(8,128)(2,1)S(1)} %dynamic-slice_bitcast_fusion.4), channel_id=1, source_target_pairs={{0,4},{4,0},{8,12},{12,8},{16,20},{20,16},{24,28},{28,24},{1,5},{5... | collective-permute-start | bytes 995336 | tf_op jit(solution)/shard_map/ppermute | solution.py:204
  (84 other events, 1170.5 us)
Sparse Core Ops, SparseCore 0:
  9.6 58.5 all-gather.10
  69.8 29.6 all-gather.12
  101.0 70.5 all-gather.14
  173.0 70.9 all-gather.16
  525.0 57.7 all-gather.20
  667.4 71.4 all-gather.18

commit v3 on v2

--- a/solution.py
+++ b/solution.py
@@ -9,7 +9,6 @@
 
 
 HIGHEST = lax.Precision.HIGHEST
-EVERY = ("seq", "mp")
 LANES = 128
 WINDOW = 256
 NT = (((1,), (1,)), ((), ()))
@@ -36,8 +35,8 @@
     return inv * (kept - mean_kept - normal * mean_both)
 
 
-def head_window(head_size, width):
-    first = pl.program_id(0) * head_size
+def head_window(head_size, width, first_head=0):
+    first = (pl.program_id(0) + first_head) * head_size
     tile = jnp.minimum(first // LANES, width // LANES - WINDOW // LANES)
     start = first - tile * LANES
     lane = lax.broadcasted_iota(jnp.int32, (1, WINDOW), 1)
@@ -94,25 +93,38 @@
     v_ref,
     g_ref,
     log_ref,
-    out_ref,
-    key_sum,
-    value_sum,
-    *,
+    *refs,
     head_size,
     rows,
+    first_head,
+    first_tile,
+    end_tile,
 ):
-    count, width = q_ref.shape
-    head = pl.program_id(0)
-    base, inside = head_window(head_size, width)
+    out_ref, key_sum, value_sum = refs[-3:]
+    count, _ = q_ref.shape
+    span_width = out_ref.shape[1] // 3
+    head = pl.program_id(0) + first_head
+    base, inside = head_window(head_size, end_tile * LANES, first_head)
     lanes = pl.ds(base, WINDOW)
     scale = head_size ** (-0.5)
     only = inside.astype(jnp.bfloat16)
     keys = k_ref[:, lanes] * only
     keys_t = keys.T
     values = v_ref[:, lanes]
+    if len(refs) == 4:
+        before = refs[0]
+        before_width = before.shape[1] // 3
+
+        @pl.when(pl.program_id(0) == 0)
+        def _():
+            for part in range(3):
+                last = (part + 1) * before_width
+                start = part * span_width
+                out_ref[:, start : start + LANES] = before[:, last - LANES : last]
 
     def put(part, mine, result):
-        there = pl.ds(pl.multiple_of(base + part * width, LANES), WINDOW)
+        there = base - first_tile * LANES + part * span_width
+        there = pl.ds(pl.multiple_of(there, LANES), WINDOW)
         out_ref[mine, there] = jnp.where(
             inside, result.astype(jnp.bfloat16), out_ref[mine, there]
         )
@@ -155,6 +167,14 @@
 
 def whole(shape):
     return pl.BlockSpec(shape, lambda n, *_: (0,) * len(shape))
+
+
+def attend_cost(heads, count, head_size, products):
+    return pl.CostEstimate(
+        flops=2 * products * heads * count * count * WINDOW,
+        transcendentals=heads * count * count,
+        bytes_accessed=2 * (products + 2) * heads * count * head_size,
+    )
 
 
 def attend(single, gates, queries, keys, values):
@@ -176,27 +196,41 @@
             jax.ShapeDtypeStruct((heads, 1, count), jnp.float32),
         ],
         name="attend",
+        cost_estimate=attend_cost(heads, count, width // heads, 2),
     )(single, gates, queries, keys, values)
 
 
-def attend_back(single, gates, queries, keys, values, grads, logs):
+def attend_back(single, gates, queries, keys, values, grads, logs, group, groups, before=None):
     count, width = queries.shape
     heads = gates.shape[1]
-    log_spec = pl.BlockSpec((1, 1, count), lambda n, *_: (n, 0, 0))
+    head_size = width // heads
+    group_heads = heads // groups
+    first_head = group * group_heads
+    first_tile = first_head * head_size // LANES
+    end_tile = -(-(first_head + group_heads) * head_size // LANES)
+    log_spec = pl.BlockSpec((1, 1, count), lambda n, *_: (n + first_head, 0, 0))
+    extra = [] if before is None else [before]
+    out_width = 3 * (end_tile - first_tile) * LANES
     return pl.pallas_call(
         lambda *refs: attend_back_kernel(
-            *refs, head_size=width // heads, rows=count // gates.shape[0]
+            *refs,
+            head_size=head_size,
+            rows=count // gates.shape[0],
+            first_head=first_head,
+            first_tile=first_tile,
+            end_tile=end_tile,
         ),
         grid_spec=pltpu.PrefetchScalarGridSpec(
             num_scalar_prefetch=2,
-            grid=(heads,),
-            in_specs=[whole((count, width))] * 4 + [log_spec],
-            out_specs=whole((count, 3 * width)),
+            grid=(group_heads,),
+            in_specs=[whole((count, width))] * 4 + [log_spec] + [whole(x.shape) for x in extra],
+            out_specs=whole((count, out_width)),
             scratch_shapes=[pltpu.VMEM((count, WINDOW), jnp.float32)] * 2,
         ),
-        out_shape=jax.ShapeDtypeStruct((count, 3 * width), jnp.bfloat16),
+        out_shape=jax.ShapeDtypeStruct((count, out_width), jnp.bfloat16),
         name="attend_back",
-    )(single, gates, queries, keys, values, grads, logs)
+        cost_estimate=attend_cost(group_heads, count, head_size, 5),
+    )(single, gates, queries, keys, values, grads, logs, *extra)
 
 
 def swap(values, axis_name, bit):
@@ -204,51 +238,80 @@
     return lax.ppermute(values, axis_name, [(i, i ^ bit) for i in range(size)])
 
 
-def pick(values, dim, major, index):
-    shape = values.shape
-    inner = shape[dim] // (2 * major)
-    cut = values.reshape(shape[:dim] + (major, 2, inner) + shape[dim + 1 :])
-    cut = lax.dynamic_index_in_dim(cut, index, dim + 1, keepdims=False)
-    return cut.reshape(shape[:dim] + (major * inner,) + shape[dim + 1 :])
-
-
-def halve(values, dim, axis_name, level, bits):
-    mine = (lax.axis_index(axis_name) >> level) & 1
-    major = 2 ** bits.index(level)
-    sent = pick(values, dim, major, 1 - mine).astype(jnp.bfloat16)
-    came = swap(sent, axis_name, 1 << level)
-    kept = pick(values, dim, major, mine)
-    bits.remove(level)
-    return kept.astype(jnp.float32) + came.astype(jnp.float32)
+def pick(values, dim, runs, index):
+    inner = values.shape[dim] // (2 * runs)
+    halves = [
+        [lax.slice_in_dim(values, (2 * r + h) * inner, (2 * r + h + 1) * inner, axis=dim) for h in (0, 1)]
+        for r in range(runs)
+    ]
+    chosen = [jnp.where(index == 1, high, low) for low, high in halves]
+    return chosen[0] if runs == 1 else jnp.concatenate(chosen, axis=dim)
 
 
 def levels_of(axis_name):
     return list(range(lax.axis_size(axis_name).bit_length() - 1))[::-1]
 
 
-def grad_sum(split_side, whole_side, split_first):
+def sum_plan():
+    steps = []
     mp_bits = levels_of("mp")
+    for level in mp_bits[::-1]:
+        steps.append((0, "mp", level, 2 ** mp_bits.index(level)))
+        mp_bits = [bit for bit in mp_bits if bit != level]
     seq_bits = levels_of("seq")
-    core = lax.axis_index("mp") & 1
-    major = 2 ** mp_bits.index(0)
-
-    def product(side):
-        if split_first:
-            return jnp.einsum("nd,ne->de", side, whole_side, preferred_element_type=jnp.float32)
-        return jnp.einsum("ne,nd->ed", whole_side, side, preferred_element_type=jnp.float32)
-
-    sent = product(pick(split_side, 1, major, 1 - core)).astype(jnp.bfloat16)
-    came = swap(sent, "mp", 1)
-    kept = product(pick(split_side, 1, major, core))
-    total = kept + came.astype(jnp.float32)
-    mp_bits.remove(0)
-    mp_dim = 0 if split_first else 1
-    for level in mp_bits[::-1]:
-        total = halve(total.astype(jnp.bfloat16), mp_dim, "mp", level, mp_bits)
-    order = [level for level in seq_bits[::-1] if level != 0] + [0]
-    for level in order:
-        total = halve(total.astype(jnp.bfloat16), 1 - mp_dim, "seq", level, seq_bits)
-    return total if split_first else total.T
+    for level in seq_bits[:-1][::-1] + [0]:
+        steps.append((1, "seq", level, 2 ** seq_bits.index(level)))
+        seq_bits = [bit for bit in seq_bits if bit != level]
+    return steps
+
+
+def column_plan():
+    levels = levels_of("seq")
+    return [(1, "seq", level, 2 ** levels.index(level)) for level in levels[::-1]]
+
+
+def my_bit(step):
+    return (lax.axis_index(step[1]) >> step[2]) & 1
+
+
+def ready(values, step):
+    return values, pick(values, step[0], step[3], 1 - my_bit(step))
+
+
+def launch(prepared, step):
+    values, sent = prepared
+    return values, swap(sent, step[1], 1 << step[2])
+
+
+def settle(pending, step, kind=jnp.bfloat16):
+    values, came = pending
+    kept = pick(values, step[0], step[3], my_bit(step))
+    return (kept.astype(jnp.float32) + came.astype(jnp.float32)).astype(kind)
+
+
+def finish(pending, plan):
+    for step, later in zip(plan[:-1], plan[1:]):
+        pending = launch(ready(settle(pending, step), later), later)
+    return settle(pending, plan[-1], jnp.float32)
+
+
+def tie(*groups):
+    return lax.optimization_barrier(groups)
+
+
+def grad_product(rows_side, cols_side):
+    product = jnp.einsum("nd,ne->de", rows_side, cols_side, preferred_element_type=jnp.float32)
+    return product.astype(jnp.bfloat16)
+
+
+def double_all(values, combine, steps):
+    for step in steps:
+        values = combine(values, swap(values, step[1], 1 << step[2]))
+    return values
+
+
+def join(mine, other):
+    return jnp.concatenate([mine, other], axis=0)
 
 
 def gelu_parts(pre):
@@ -286,7 +349,6 @@
     group_count = chan_mask.shape[1]
     hidden_width = up_bias.shape[0]
     mp_size = lax.axis_size("mp")
-    seq_size = lax.axis_size("seq")
     slot_rows = row_count // slot_count
     blocked = (slot_count, slot_rows, model_width)
     flat = (row_count, model_width)
@@ -342,36 +404,49 @@
     second_in = (second_normal * (1.0 + second_scale) + second_shift).astype(jnp.bfloat16)
     second_in = second_in.reshape(flat)
 
+    grad_final = cotangent.astype(jnp.float32).reshape(blocked)
+    grad_out = (keep_rows * second_gate * grad_final).astype(jnp.bfloat16).reshape(flat)
+    down_bias_grad = jnp.sum(grad_out.astype(jnp.float32), axis=0)
+    plan = sum_plan()
+    core, across = plan[0], plan[1]
+    mp_steps = len(levels_of("mp"))
+
     pre_act = jnp.dot(second_in, full_up, preferred_element_type=jnp.float32) + up_bias.astype(
         jnp.float32
     )
     value, slope = gelu_parts(pre_act.reshape(slot_count, slot_rows, hidden_width))
     hidden = (value * unit_gate).astype(jnp.bfloat16).reshape(row_count, hidden_width)
+
+    down_sum = ready(grad_product(hidden, grad_out), core)
+    hidden, down_sum = tie(hidden, down_sum)
+    down_sum = launch(down_sum, core)
     mlp_out = (
         jnp.dot(hidden, full_down, preferred_element_type=jnp.float32)
         + down_bias.astype(jnp.float32)
     ).astype(jnp.bfloat16)
     mlp_float = mlp_out.astype(jnp.float32).reshape(blocked)
     output = (middle + keep_rows * second_gate * mlp_float).astype(jnp.bfloat16).reshape(flat)
-
-    grad_final = cotangent.astype(jnp.float32).reshape(blocked)
-    grad_out = (keep_rows * second_gate * grad_final).astype(jnp.bfloat16).reshape(flat)
     grad_second_gate = jnp.sum(keep_rows * grad_final * mlp_float, axis=1)
+
+    down_sum = ready(settle(down_sum, core), across)
+    grad_out, down_sum = tie(grad_out, down_sum)
+    down_sum = launch(down_sum, across)
     grad_hidden = jnp.einsum(
         "nd,fd->nf", grad_out, full_down, preferred_element_type=jnp.float32
     ).reshape(slot_count, slot_rows, hidden_width)
     grad_pre = (grad_hidden * unit_gate * slope).astype(jnp.bfloat16)
     grad_pre = grad_pre.reshape(row_count, hidden_width)
-    down_piece = grad_sum(hidden, grad_out, False)
-    grad_second = (
-        jnp.einsum("nf,df->nd", grad_pre, full_up, preferred_element_type=jnp.float32)
-        .astype(jnp.bfloat16)
-        .astype(jnp.float32)
-        .reshape(blocked)
-    )
-    up_piece = grad_sum(second_in, grad_pre, True)
     up_bias_grad = jnp.sum(grad_pre.astype(jnp.float32), axis=0)
-    down_bias_grad = jnp.sum(grad_out.astype(jnp.float32), axis=0)
+
+    up_sum = ready(grad_product(second_in, grad_pre), core)
+    grad_pre, up_sum = tie(grad_pre, up_sum)
+    up_sum = launch(up_sum, core)
+    grad_second = jnp.einsum("nf,df->nd", grad_pre, full_up, preferred_element_type=jnp.float32)
+    grad_second = grad_second.astype(jnp.bfloat16)
+    up_sum = ready(settle(up_sum, core), across)
+    grad_second, up_sum = tie(grad_second, up_sum)
+    up_sum = launch(up_sum, across)
+    grad_second = grad_second.astype(jnp.float32).reshape(blocked)
 
     grad_second_scale = jnp.sum(grad_second * second_normal, axis=1)
     grad_second_shift = jnp.sum(grad_second, axis=1)
@@ -383,72 +458,125 @@
     grad_cat = jnp.einsum(
         "ne,de->nd", grad_branch, full_proj, preferred_element_type=jnp.float32
     ).astype(jnp.bfloat16)
-    proj_piece = grad_sum(attn_cat, grad_branch, False)
+    proj_sum = ready(grad_product(attn_cat, grad_branch), core)
     proj_bias_grad = jnp.sum(grad_branch.astype(jnp.float32), axis=0)
-
-    lone = jnp.arange(slot_count)[:, None] == 0
-
-    def per_item(sums):
-        return jnp.where(single, jnp.where(lone, jnp.sum(sums, axis=0, keepdims=True), 0.0), sums)
-
-    early = per_item(
-        jnp.concatenate(
-            [grad_first_gate, grad_second_shift, grad_second_scale, grad_second_gate], axis=1
+    down_sum = ready(settle(down_sum, across), plan[2])
+    grad_cat, proj_sum, down_sum = tie(grad_cat, proj_sum, down_sum)
+    proj_sum = launch(proj_sum, core)
+    down_sum = launch(down_sum, plan[2])
+
+    attn_args = (lone_flag, gates, queries, keys_all, values_all)
+    low_part = attend_back(*attn_args, grad_cat, log_total, 0, 2)
+    low_width = low_part.shape[1] // 3
+    low_done = low_width - LANES
+    low_cols = jnp.concatenate(
+        [low_part[:, part * low_width : part * low_width + low_done] for part in range(3)], axis=1
+    )
+    low_sum = ready(grad_product(normed, low_cols), core)
+    down_sum = ready(settle(down_sum, plan[2]), plan[3])
+    up_sum = ready(settle(up_sum, across), plan[2])
+    proj_sum = ready(settle(proj_sum, core), across)
+    low_part, low_sum, down_sum, up_sum, proj_sum = tie(
+        low_part, low_sum, down_sum, up_sum, proj_sum
+    )
+    low_sum = launch(low_sum, core)
+    proj_sum = launch(proj_sum, across)
+    up_sum = launch(up_sum, plan[2])
+    down_sum = launch(down_sum, plan[3])
+
+    high_cols = attend_back(*attn_args, grad_cat, log_total, 1, 2, low_part)
+    high_width = high_cols.shape[1] // 3
+    low_sum = ready(settle(low_sum, core), across)
+    high_cols, low_sum = tie(high_cols, low_sum)
+    low_sum = launch(low_sum, across)
+    high_sum = ready(grad_product(normed, high_cols), core)
+    high_cols, high_sum = tie(high_cols, high_sum)
+    up_sum = ready(settle(up_sum, plan[2]), plan[3])
+    proj_sum = ready(settle(proj_sum, across), plan[2])
+    down_sum = ready(settle(down_sum, plan[3]), plan[4])
+    high_sum = launch(high_sum, core)
+
+    def interleave(low, high):
+        return jnp.concatenate(
+            [
+                piece
+                for part in range(3)
+                for piece in (
+                    low[:, part * low_done : (part + 1) * low_done],
+                    high[:, part * high_width : (part + 1) * high_width],
+                )
+            ],
+            axis=1,
         )
-    )
-    rest = jnp.zeros((early.shape[1] - 2 * model_width - slot_count,), jnp.float32)
-    early_rows = jnp.concatenate(
-        [
-            early,
-            up_bias_grad[None, :],
-            jnp.concatenate([down_bias_grad, proj_bias_grad, stamp_float, rest])[None, :],
-        ],
-        axis=0,
-    )
-    all_early = lax.all_gather(early_rows, EVERY, axis=0, tiled=False)
-    grad_joined = attend_back(
-        lone_flag, gates, queries, keys_all, values_all, grad_cat, log_total
-    )
+
+    grad_joined = interleave(low_cols, high_cols)
+    high_sum = ready(settle(high_sum, core), across)
+    grad_joined, high_sum, up_sum, proj_sum, down_sum = tie(
+        grad_joined, high_sum, up_sum, proj_sum, down_sum
+    )
+    high_sum = launch(high_sum, across)
+    up_sum = launch(up_sum, plan[3])
+    proj_sum = launch(proj_sum, plan[2])
+    down_sum = launch(down_sum, plan[4])
     grad_normed = jnp.einsum("ne,de->nd", grad_joined, full_qkv, preferred_element_type=jnp.float32)
-    qkv_piece = grad_sum(normed, grad_joined, False)
     column_sums = jnp.sum(grad_joined.astype(jnp.float32), axis=0)
     qv_bias_grad = jnp.concatenate([column_sums[:model_width], column_sums[2 * model_width :]])
+    qkv_sum = interleave(settle(low_sum, across), settle(high_sum, across))
+    qkv_sum = ready(qkv_sum, plan[2])
+    grad_normed, qkv_sum = tie(grad_normed, qkv_sum)
+    qkv_sum = launch(qkv_sum, plan[2])
+
     grad_normed = grad_normed.reshape(blocked)
-    token_grad = grad_middle + norm_back(
-        grad_normed * (1.0 + first_scale), first_inv, first_normal
-    )
+    token_grad = grad_middle + norm_back(grad_normed * (1.0 + first_scale), first_inv, first_normal)
     grad_first_scale = jnp.sum(grad_normed * first_normal, axis=1)
     grad_first_shift = jnp.sum(grad_normed, axis=1)
-    late = per_item(jnp.concatenate([grad_first_shift, grad_first_scale], axis=1))
-    late_rows = jnp.concatenate([late, qv_bias_grad[None, :]], axis=0)
-    all_late = lax.all_gather(late_rows, EVERY, axis=0, tiled=False)
-
-    item_count = slot_count * mp_size * seq_size
-    all_modulation = jnp.concatenate(
-        [all_late[:, :slot_count], all_early[:, :slot_count]], axis=2
-    ).reshape(item_count, 6 * model_width)
-    all_stamps = all_early[:, slot_count + 1, 2 * model_width : 2 * model_width + slot_count]
-    cond_cols = condition_of(all_stamps.reshape(item_count)).astype(jnp.float32)
-    col_width = 6 * model_width // seq_size
-    mod_cols = lax.dynamic_slice_in_dim(
-        all_modulation, lax.axis_index("seq") * col_width, col_width, 1
-    )
+
+    lone = jnp.arange(slot_count)[:, None] == 0
+    sums = jnp.concatenate(
+        [
+            grad_first_shift,
+            grad_first_scale,
+            grad_first_gate,
+            grad_second_shift,
+            grad_second_scale,
+            grad_second_gate,
+        ],
+        axis=1,
+    )
+    grad_modulation = jnp.where(
+        single, jnp.where(lone, jnp.sum(sums, axis=0, keepdims=True), 0.0), sums
+    )
+    biases = jnp.concatenate(
+        [
+            jnp.sum(grad_modulation, axis=0),
+            qv_bias_grad,
+            proj_bias_grad,
+            up_bias_grad,
+            down_bias_grad,
+        ]
+    )
+    mp_plan = plan[:mp_steps]
+    near_plan = column_plan()
+    biases = double_all(biases, jnp.add, mp_plan + near_plan)
+    mod_cols = grad_modulation
+    for step in near_plan:
+        kept, sent = ready(mod_cols, step)
+        other = swap(sent, step[1], 1 << step[2])
+        mod_cols = join(pick(kept, step[0], step[3], my_bit(step)), other)
+    mod_cols = double_all(mod_cols, join, mp_plan)
+    all_stamps = double_all(stamp_float, join, near_plan + mp_plan)
+    cond_cols = condition_of(all_stamps).astype(jnp.float32)
     ada_piece = jnp.einsum("sd,sc->dc", cond_cols, mod_cols, precision=HIGHEST)
-    ada_bias_grad = jnp.sum(all_modulation, axis=0)
-    early_bias = jnp.sum(all_early[:, slot_count:], axis=0)
+    ends = [6 * model_width, 8 * model_width, 9 * model_width, 9 * model_width + hidden_width]
     return (
         output,
         token_grad.reshape(flat),
         ada_piece,
-        qkv_piece,
-        proj_piece,
-        up_piece,
-        down_piece.reshape(hidden_width // mp_size, model_width // seq_size),
-        ada_bias_grad,
-        jnp.sum(all_late[:, slot_count], axis=0),
-        early_bias[1, model_width : 2 * model_width],
-        early_bias[0],
-        early_bias[1, :model_width],
+        finish(qkv_sum, plan[2:]),
+        finish(proj_sum, plan[2:]),
+        finish(up_sum, plan[3:]),
+        finish(down_sum, plan[4:]),
+        *jnp.split(biases, ends),
     )
 
 
@@ -486,6 +614,7 @@
         P(),
         P(),
     )
+
     return jax.shard_map(
         on_device, mesh=mesh, in_specs=in_specs, out_specs=out_specs, check_vma=False
     )

time: 1010 us -> 770 us (0.76)
  local copies, waits for them, and re-layouts: 324 us -> 65.7 us
  Pallas kernels: 141 us -> 75.1 us
  starting transfers between devices: 23 us -> 81 us
  waiting for transfers between devices: 152 us -> 204 us
  matrix products: 205 us -> 185 us
    reshape x21 -> x0, local copies, waits for them, and re-layouts: 94.6 us -> none  [the longest x2 50.3 us: on_device(): pre_act.reshape(slot_count, slot_rows, hidden_width)]
    mul x4 -> x1, local copies, waits for them, and re-layouts: 59.3 us -> 0.13 us  [on_device(): value * unit_gate]
    ppermute x26 -> x43, starting transfers between devices: 22.7 us -> 80.8 us  [swap(): return lax.ppermute(values, axis_name, [(i, i ^ bit) for i in range(size)])]
    dynamic_slice x10 -> x0, local copies, waits for them, and re-layouts: 56.9 us -> none  [pick(): cut = lax.dynamic_index_in_dim(cut, index, dim + 1, keepdims=False)]
    select_n x2 -> x35, other arithmetic: 0.16 us -> 45.4 us  [pick(): chosen = [jnp.where(index == 1, high, low) for low, high in halves]]
    all_gather x1, waiting for transfers between devices: 0.01 us -> 43.6 us  [on_device(): full_up = lax.all_gather(up_weight, 'mp', axis=0, tiled=True)]
    pallas_call x1 -> x2, Pallas kernels: 86.6 us -> 48.5 us  [attend_back(): pl.pallas_call(lambda *refs: attend_back_kernel(*refs, head_size=head_siz...]
    mul x7 -> x0, local copies, waits for them, and re-layouts: 31.9 us -> none  [the longest x2 10.9 us: on_device(): middle = tok_float + first_gate * branch]
  transfers between devices with their start and end apart: 32 -> 47, of which waited for: 11 -> 20; matrix products, arithmetic and copies ran while one was open for 55% -> 37% of each run, Pallas kernels for 5% -> 10%
where the time goes in v3:
time: 770 us; the launch traced here: 764 us
  waiting for transfers between devices  204 us (26%)
  matrix products  185 us (24%)
  other arithmetic  137 us (18%)
  starting transfers between devices  81 us (11%)
  Pallas kernels  75.1 us (10%)
  local copies, waits for them, and re-layouts  65.7 us (9%)
  between operations  16.6 us (2%)
    ppermute x43, waiting for transfers between devices, swap(): return lax.ppermute(values, axis_name, [(i, i ^ bit) for i in range(size)])  132 us
    ppermute x43, starting transfers between devices, swap(): return lax.ppermute(values, axis_name, [(i, i ^ bit) for i in range(size)])  80.8 us
    pallas_call x2, Pallas kernels, attend_back(): pl.pallas_call(lambda *refs: attend_back_kernel(*refs, head_size=head_siz...  48.5 us
    select_n x35, other arithmetic, pick(): chosen = [jnp.where(index == 1, high, low) for low, high in halves]  45.4 us
    all_gather x1, waiting for transfers between devices, on_device(): full_up = lax.all_gather(up_weight, 'mp', axis=0, tiled=True)  43.6 us
    dot_general x5, matrix products, grad_product(): jnp.einsum('nd,ne->de', rows_side, cols_side, preferred_element_type=jnp....  43.6 us
    unnamed x225, local copies, waits for them, and re-layouts  34.6 us
    convert_element_type x18, other arithmetic, settle(): return (kept.astype(jnp.float32) + came.astype(jnp.float32)).astype(kind)  34 us
  transfers between devices with their start and end apart: 47, of which 20 were waited for; matrix products, arithmetic and copies ran while one was open for 37% of the time, Pallas kernels for 10%

profile of v3, /device:TPU:0, one launch (start us, length us, event | category | flops | bytes accessed | tf_op | source)
XLA Modules:
  0.0 764.3 jit_solution(14817991509733079285)
XLA Ops:
  46.5 26.5 %all-gather.5.cloned.1.call-done = bf16[1152,3456]{1,0:T(8,128)(2,1)} async-done(((bf16[288,3456]{1,0:T(8,128)(2,1)}), bf16[1152,3456]{1,0:T(8,128)(2,1)}) %all-gather.5.cloned.1.call-update) | async-done | bytes 7962640 | tf_op jit(solution)/shard_map/all_gather | solution.py:373
  72.9 13.5 %fusion.68 = f32[1024,3456]{1,0:T(8,128)S(1)} fusion(bf16[1024,1152]{1,0:T(8,128)(2,1)} %fusion.6, bf16[1152,3456]{1,0:T(8,128)(2,1)} %all-gather.5.cloned.1.call-done), kind=kOutput, calls=%fused_computation.273 | convolution fusion | flops 8153726976 | bytes 24477696 | tf_op jit(solution)/shard_map/dot_general | solution.py:390
  91.1 26.6 %attend.1 = (bf16[1024,1152]{1,0:T(8,128)(2,1)}, f32[16,1,1024]{2,1,0:T(1,128)}) custom-call(s32[1]{0:T(128)S(6)} %reshape.279.refs_0_, s32[4,16]{1,0:T(4,128)} %broadcast_select_fusion.10.refs_1_, bf16[1024,1152]{1,0:T(8,128)(2,1)} %get-tuple-element.152.refs_2_, bf16[1024,1152]{1,0:T(8,128)(2,1)} %slice.993.refs_3_, ...), custom_call_target="tpu_custom_call" | custom-call | flops 17179869184 | bytes 9437184 | tf_op jit(solution)/shard_map/attend/pallas_call | solution.py:184
  129.1 43.6 %all-gather.9.cloned.1.call-done = bf16[1152,4608]{1,0:T(8,128)(2,1)} async-done(((bf16[288,4608]{1,0:T(8,128)(2,1)}), bf16[1152,4608]{1,0:T(8,128)(2,1)}) %all-gather.9.cloned.1.call-update) | async-done | bytes 10616848 | tf_op jit(solution)/shard_map/all_gather | solution.py:375
  172.7 22.0 %fusion = (bf16[1024,4608]{1,0:T(8,128)(2,1)S(1)}, f32[1024,4608]{1,0:T(8,128)}) fusion(f32[4,4608]{1,0:T(4,128)S(1)} %mul.390, f32[4608]{0:T(1024)S(1)} %convert_element_type.327, bf16[1024,1152]{1,0:T(8,128)(2,1)S(1)} %fusion.8, bf16[1152,4608]{1,0:T(8,128)(2,1)} %all-gather.9.cloned.1.call-done), kind=kOutput, calls=%fused_computation.4 | convolution fusion | flops 10923540480 | bytes 41379840 | tf_op jit(solution)/shard_map/dot_general | solution.py:414
  194.8 16.9 %convolution_convert_fusion.1 = bf16[4608,1152]{1,0:T(8,128)(2,1)S(1)} fusion(bf16[1024,4608]{1,0:T(8,128)(2,1)S(1)} %get-tuple-element.59, bf16[1024,1152]{1,0:T(8,128)(2,1)} %get-tuple-element.62), kind=kOutput, calls=%fused_computation.3 | convolution fusion | flops 10876944384 | bytes 22413312 | tf_op jit(solution)/shard_map/nd,ne->de/dot_general | solution.py:303
  253.5 28.0 %convert_reduce_fusion = (f32[4608]{0:T(1024)}, bf16[1024,4608]{1,0:T(8,128)(2,1)S(1)}) fusion(f32[1024,4608]{1,0:T(8,128)} %get-tuple-element.236, f32[4608]{0:T(1024)S(1)} %convert_element_type.327, f32[4,4608]{1,0:T(4,128)S(1)} %mul.390, bf16[1024,1152]{1,0:T(8,128)(2,1)} %get-tuple-element.62, bf16[4608,1152]{1,0:T(8,128)(2,1)} %all-gather.11.cloned.1.call-done), kind=kOutput, calls=%fused_computation.7 | convolution fusion | flops 10975440896 | bytes 41398272 | tf_op jit(solution)/shard_map/nd,fd->nf/dot_general | solution.py:434
  285.0 11.9 %convolution_convert_fusion = bf16[1152,4608]{1,0:T(8,128)(2,1)S(1)} fusion(bf16[1024,1152]{1,0:T(8,128)(2,1)S(1)} %copy-done.22, bf16[1024,4608]{1,0:T(8,128)(2,1)S(1)} %get-tuple-element.63), kind=kOutput, calls=%fused_computation.2 | convolution fusion | flops 10876944384 | bytes 22413312 | tf_op jit(solution)/shard_map/nd,ne->de/dot_general | solution.py:303
  310.5 19.0 %convolution_convert_fusion.5 = bf16[1024,1152]{1,0:T(8,128)(2,1)} fusion(bf16[1024,4608]{1,0:T(8,128)(2,1)} %copy-done.23, bf16[1152,4608]{1,0:T(8,128)(2,1)} %all-gather.9.cloned.1.call-done), kind=kOutput, calls=%fused_computation.69 | convolution fusion | flops 10872815616 | bytes 22413312 | tf_op jit(solution)/shard_map/nf,df->nd/dot_general | solution.py:444
  350.3 25.0 %convert_reduce_fusion.3 = (f32[1152]{0:T(1024)}, bf16[1024,1152]{1,0:T(8,128)(2,1)S(1)}, f32[1024,1152]{1,0:T(8,128)}, bf16[1024,1152]{1,0:T(8,128)(2,1)}, f32[1024,1152]{1,0:T(8,128)}) fusion(f32[4,1152]{1,0:T(4,128)S(1)} %get-tuple-element.223, f32[1024]{0:T(1024)S(1)} %get-tuple-element.240, f32[1024,1152]{1,0:T(8,128)} %copy-done, ...), kind=kOutput, calls=%fused_computation.50 | convolution fusion | flops 10896407552 | bytes 43731968 | tf_op jit(solution)/shard_map/dot_general | solution.py:424
  395.2 23.6 %attend_back.2.refs_7_ = bf16[1024,1920]{1,0:T(8,128)(2,1)} custom-call(s32[1]{0:T(128)S(6)} %reshape.279.refs_0_, s32[4,16]{1,0:T(4,128)} %broadcast_select_fusion.10.refs_1_, bf16[1024,1152]{1,0:T(8,128)(2,1)} %get-tuple-element.152.refs_2_, bf16[1024,1152]{1,0:T(8,128)(2,1)} %slice.993.refs_3_, bf16[1024,1152]{1,0:T(8,128)(2,1)} %get-tuple-element.151.refs_4_, ...), custom_call_target="tpu_custom_call" | custom-call | flops 21474836480 | bytes 8257536 | tf_op jit(solution)/shard_map/attend_back/pallas_call | solution.py:214
  440.1 9.1 %collective-permute-done.10 = bf16[288,4608]{1,0:T(8,128)(2,1)} collective-permute-done((bf16[288,4608]{1,0:T(8,128)(2,1)}, bf16[288,4608]{1,0:T(8,128)(2,1)}, u32[]{:S(2)}, u32[]{:S(2)}) %collective-permute-start.10) | collective-permute-done | bytes 2654240 | tf_op jit(solution)/shard_map/ppermute | solution.py:238
  454.8 24.9 %attend_back.3 = bf16[1024,1920]{1,0:T(8,128)(2,1)} custom-call(s32[1]{0:T(128)S(6)} %reshape.279.refs_0_, s32[4,16]{1,0:T(4,128)} %broadcast_select_fusion.10.refs_1_, bf16[1024,1152]{1,0:T(8,128)(2,1)} %get-tuple-element.152.refs_2_, bf16[1024,1152]{1,0:T(8,128)(2,1)} %slice.993.refs_3_, bf16[1024,1152]{1,0:T(8,128)(2,1)} %get-tuple-element.151.refs_4_, ...), custom_call_target="tpu_custom_call" | custom-call | flops 21474836480 | bytes 8257536 | tf_op jit(solution)/shard_map/attend_back/pallas_call | solution.py:214
  480.8 15.3 %collective-permute-start.16 = (bf16[1152,288]{0,1:T(8,128)(2,1)}, bf16[1152,288]{0,1:T(8,128)(2,1)}, u32[]{:S(2)}, u32[]{:S(2)}) collective-permute-start(bf16[1152,288]{0,1:T(8,128)(2,1)} %copy.33), channel_id=1, source_target_pairs={{0,16},{4,20},{8,24},{12,28},{16,0},{20,4},{24,8},{28,12},{1,17},{... | collective-permute-start | bytes 1990664 | tf_op jit(solution)/shard_map/ppermute | solution.py:238
  496.1 23.7 %collective-permute-start.15 = (bf16[288,1152]{1,0:T(8,128)(2,1)}, bf16[288,1152]{1,0:T(8,128)(2,1)S(1)}, u32[]{:S(2)}, u32[]{:S(2)}) collective-permute-start(bf16[288,1152]{1,0:T(8,128)(2,1)} %slice_select_fusion.26), channel_id=1, source_target_pairs={{0,2},{1,3},{2,0},{3,1},{4,6},{5,7},{6,4},{7,5},{8,10},{9,11},{10,... | collective-permute-start | bytes 1990664 | tf_op jit(solution)/shard_map/ppermute | solution.py:238
  526.0 9.4 %collective-permute-done.15 = bf16[288,1152]{1,0:T(8,128)(2,1)S(1)} collective-permute-done((bf16[288,1152]{1,0:T(8,128)(2,1)}, bf16[288,1152]{1,0:T(8,128)(2,1)S(1)}, u32[]{:S(2)}, u32[]{:S(2)}) %collective-permute-start.15) | collective-permute-done | bytes 663584 | tf_op jit(solution)/shard_map/ppermute | solution.py:238
  540.4 18.0 %collective-permute-done.14 = bf16[288,2304]{1,0:T(8,128)(2,1)} collective-permute-done((bf16[288,2304]{1,0:T(8,128)(2,1)}, bf16[288,2304]{1,0:T(8,128)(2,1)}, u32[]{:S(2)}, u32[]{:S(2)}) %collective-permute-start.14) | collective-permute-done | bytes 1327136 | tf_op jit(solution)/shard_map/ppermute | solution.py:238
  563.2 9.2 %collective-permute-start.17 = (bf16[288,1536]{1,0:T(8,128)(2,1)S(1)}, bf16[288,1536]{1,0:T(8,128)(2,1)S(1)}, u32[]{:S(2)}, u32[]{:S(2)}) collective-permute-start(bf16[288,1536]{1,0:T(8,128)(2,1)S(1)} %slice_select_fusion.15), channel_id=1, source_target_pairs={{0,2},{1,3},{2,0},{3,1},{4,6},{5,7},{6,4},{7,5},{8,10},{9,11},{10,... | collective-permute-start | bytes 2654216 | tf_op jit(solution)/shard_map/ppermute | solution.py:238
  581.0 11.0 %collective-permute-done.17 = bf16[288,1536]{1,0:T(8,128)(2,1)S(1)} collective-permute-done((bf16[288,1536]{1,0:T(8,128)(2,1)S(1)}, bf16[288,1536]{1,0:T(8,128)(2,1)S(1)}, u32[]{:S(2)}, u32[]{:S(2)}) %collective-permute-start.17) | collective-permute-done | bytes 884768 | tf_op jit(solution)/shard_map/ppermute | solution.py:238
  610.6 15.9 %fusion.69 = f32[1024,1152]{1,0:T(8,128)} fusion(bf16[1024,3456]{1,0:T(8,128)(2,1)} %copy-done.24, bf16[1152,3456]{1,0:T(8,128)(2,1)} %all-gather.5.cloned.1.call-done), kind=kOutput, calls=%fused_computation.274 | convolution fusion | flops 8153726976 | bytes 19759104 | tf_op jit(solution)/shard_map/ne,de->nd/dot_general | solution.py:521
  628.5 14.4 %collective-permute-done.33 = bf16[288,288]{1,0:T(8,128)(2,1)} collective-permute-done((bf16[288,288]{1,0:T(8,128)(2,1)}, bf16[288,288]{1,0:T(8,128)(2,1)}, u32[]{:S(2)}, u32[]{:S(2)}) %collective-permute-start.33) | collective-permute-done | bytes 165920 | tf_op jit(solution)/shard_map/ppermute | solution.py:238
  696.5 15.3 %collective-permute-done.25 = f32[8,1728]{1,0:T(8,128)S(1)} collective-permute-done((f32[8,1728]{1,0:T(8,128)S(1)}, f32[8,1728]{1,0:T(8,128)S(1)}, u32[]{:S(2)}, u32[]{:S(2)}) %collective-permute-start.25) | collective-permute-done | bytes 55328 | tf_op jit(solution)/shard_map/ppermute | solution.py:238
  716.7 12.5 %collective-permute-done.26 = f32[16,864]{1,0:T(8,128)S(1)} collective-permute-done((f32[16,864]{1,0:T(8,128)S(1)}, f32[16,864]{1,0:T(8,128)S(1)}, u32[]{:S(2)}, u32[]{:S(2)}) %collective-permute-start.26) | collective-permute-done | bytes 55328 | tf_op jit(solution)/shard_map/ppermute | solution.py:238
  732.5 8.7 %collective-permute-done.41 = f32[16128]{0:T(1024)S(1)} collective-permute-done((f32[16128]{0:T(1024)S(1)}, f32[16128]{0:T(1024)S(1)}, u32[]{:S(2)}, u32[]{:S(2)}) %collective-permute-start.41) | collective-permute-done | bytes 64544 | tf_op jit(solution)/shard_map/ppermute | solution.py:238
  (476 shorter events, 303.9 us)
Async XLA Ops:
  7.2 65.7 %all-gather.5.cloned.1.call-start = ((), (), s32[]{:S(2)}) async-start(), calls=%async_computation | async-start | bytes 9953280 | tf_op jit(solution)/shard_map/all_gather | solution.py:373
  7.9 109.7 %all-gather.7.cloned.1.call-start = ((), (), s32[]{:S(2)}) async-start(), calls=%async_computation.1 | async-start | bytes 3317760 | tf_op jit(solution)/shard_map/all_gather | solution.py:374
  8.7 164.1 %all-gather.9.cloned.1.call-start = ((), (), s32[]{:S(2)}) async-start(), calls=%async_computation.2 | async-start | bytes 13271040 | tf_op jit(solution)/shard_map/all_gather | solution.py:375
  9.4 244.0 %all-gather.11.cloned.1.call-start = ((), (), s32[]{:S(2)}) async-start(), calls=%async_computation.3 | async-start | bytes 13271040 | tf_op jit(solution)/shard_map/all_gather | solution.py:376
  222.6 22.6 %collective-permute-start.6 = (bf16[2304,1152]{1,0:T(8,128)(2,1)}, bf16[2304,1152]{1,0:T(8,128)(2,1)}, u32[]{:S(2)}, u32[]{:S(2)}) collective-permute-start(bf16[2304,1152]{1,0:T(8,128)(2,1)} %pad_maximum_fusion), channel_id=1, source_target_pairs={{0,1},{1,0},{2,3},{3,2},{4,5},{5,4},{6,7},{7,6},{8,9},{9,8},{10,11... | collective-permute-start | bytes 15925256 | tf_op jit(solution)/shard_map/ppermute | solution.py:238
  253.1 76.4 %collective-permute-start.8 = (bf16[1152,1152]{1,0:T(8,128)(2,1)}, bf16[1152,1152]{1,0:T(8,128)(2,1)}, u32[]{:S(2)}, u32[]{:S(2)}) collective-permute-start(bf16[1152,1152]{1,0:T(8,128)(2,1)} %slice_select_fusion.3), channel_id=1, source_target_pairs={{0,2},{1,3},{2,0},{3,1},{4,6},{5,7},{6,4},{7,5},{8,10},{9,11},{10,... | collective-permute-start | bytes 7962632 | tf_op jit(solution)/shard_map/ppermute | solution.py:238
  303.7 31.1 %collective-permute-start.7 = (bf16[576,4608]{1,0:T(8,128)(2,1)}, bf16[576,4608]{1,0:T(8,128)(2,1)}, u32[]{:S(2)}, u32[]{:S(2)}) collective-permute-start(bf16[576,4608]{1,0:T(8,128)(2,1)} %pad_maximum_fusion.1), channel_id=1, source_target_pairs={{0,1},{1,0},{2,3},{3,2},{4,5},{5,4},{6,7},{7,6},{8,9},{9,8},{10,11... | collective-permute-start | bytes 15925256 | tf_op jit(solution)/shard_map/ppermute | solution.py:238
  388.9 45.9 %collective-permute-start.11 = (bf16[576,1152]{1,0:T(8,128)(2,1)}, bf16[576,1152]{1,0:T(8,128)(2,1)}, u32[]{:S(2)}, u32[]{:S(2)}) collective-permute-start(bf16[576,1152]{1,0:T(8,128)(2,1)} %pad_maximum_fusion.5), channel_id=1, source_target_pairs={{0,1},{1,0},{2,3},{3,2},{4,5},{5,4},{6,7},{7,6},{8,9},{9,8},{10,11... | collective-permute-start | bytes 3981320 | tf_op jit(solution)/shard_map/ppermute | solution.py:238
  389.4 59.8 %collective-permute-start.10 = (bf16[288,4608]{1,0:T(8,128)(2,1)}, bf16[288,4608]{1,0:T(8,128)(2,1)}, u32[]{:S(2)}, u32[]{:S(2)}) collective-permute-start(bf16[288,4608]{1,0:T(8,128)(2,1)} %slice_select_fusion), channel_id=1, source_target_pairs={{0,2},{1,3},{2,0},{3,1},{4,6},{5,7},{6,4},{7,5},{8,10},{9,11},{10,... | collective-permute-start | bytes 7962632 | tf_op jit(solution)/shard_map/ppermute | solution.py:238
  393.7 38.7 %collective-permute-start.9 = (bf16[1152,576]{0,1:T(8,128)(2,1)}, bf16[1152,576]{0,1:T(8,128)(2,1)}, u32[]{:S(2)}, u32[]{:S(2)}) collective-permute-start(bf16[1152,576]{0,1:T(8,128)(2,1)} %copy.31), channel_id=1, source_target_pairs={{0,8},{4,12},{8,0},{12,4},{16,24},{20,28},{24,16},{28,20},{1,9},{5... | collective-permute-start | bytes 3981320 | tf_op jit(solution)/shard_map/ppermute | solution.py:238
  454.8 106.2 %collective-permute-start.12 = (bf16[576,1536]{1,0:T(8,128)(2,1)}, bf16[576,1536]{1,0:T(8,128)(2,1)}, u32[]{:S(2)}, u32[]{:S(2)}) collective-permute-start(bf16[576,1536]{1,0:T(8,128)(2,1)} %pad_maximum_fusion.3), channel_id=1, source_target_pairs={{0,1},{1,0},{2,3},{3,2},{4,5},{5,4},{6,7},{7,6},{8,9},{9,8},{10,11... | collective-permute-start | bytes 5308424 | tf_op jit(solution)/shard_map/ppermute | solution.py:238
  480.8 43.6 %collective-permute-start.16 = (bf16[1152,288]{0,1:T(8,128)(2,1)}, bf16[1152,288]{0,1:T(8,128)(2,1)}, u32[]{:S(2)}, u32[]{:S(2)}) collective-permute-start(bf16[1152,288]{0,1:T(8,128)(2,1)} %copy.33), channel_id=1, source_target_pairs={{0,16},{4,20},{8,24},{12,28},{16,0},{20,4},{24,8},{28,12},{1,17},{... | collective-permute-start | bytes 1990664 | tf_op jit(solution)/shard_map/ppermute | solution.py:238
  496.1 39.3 %collective-permute-start.15 = (bf16[288,1152]{1,0:T(8,128)(2,1)}, bf16[288,1152]{1,0:T(8,128)(2,1)S(1)}, u32[]{:S(2)}, u32[]{:S(2)}) collective-permute-start(bf16[288,1152]{1,0:T(8,128)(2,1)} %slice_select_fusion.26), channel_id=1, source_target_pairs={{0,2},{1,3},{2,0},{3,1},{4,6},{5,7},{6,4},{7,5},{8,10},{9,11},{10,... | collective-permute-start | bytes 1990664 | tf_op jit(solution)/shard_map/ppermute | solution.py:238
  523.1 35.2 %collective-permute-start.14 = (bf16[288,2304]{1,0:T(8,128)(2,1)}, bf16[288,2304]{1,0:T(8,128)(2,1)}, u32[]{:S(2)}, u32[]{:S(2)}) collective-permute-start(bf16[288,2304]{1,0:T(8,128)(2,1)} %pad_maximum_fusion.6), channel_id=1, source_target_pairs={{0,8},{4,12},{8,0},{12,4},{16,24},{20,28},{24,16},{28,20},{1,9},{5... | collective-permute-start | bytes 3981320 | tf_op jit(solution)/shard_map/ppermute | solution.py:238
  563.2 28.8 %collective-permute-start.17 = (bf16[288,1536]{1,0:T(8,128)(2,1)S(1)}, bf16[288,1536]{1,0:T(8,128)(2,1)S(1)}, u32[]{:S(2)}, u32[]{:S(2)}) collective-permute-start(bf16[288,1536]{1,0:T(8,128)(2,1)S(1)} %slice_select_fusion.15), channel_id=1, source_target_pairs={{0,2},{1,3},{2,0},{3,1},{4,6},{5,7},{6,4},{7,5},{8,10},{9,11},{10,... | collective-permute-start | bytes 2654216 | tf_op jit(solution)/shard_map/ppermute | solution.py:238
  595.4 65.2 %collective-permute-start.18 = (bf16[288,1920]{1,0:T(8,128)(2,1)}, bf16[288,1920]{1,0:T(8,128)(2,1)}, u32[]{:S(2)}, u32[]{:S(2)}) collective-permute-start(bf16[288,1920]{1,0:T(8,128)(2,1)} %slice_select_fusion.10), channel_id=1, source_target_pairs={{0,2},{1,3},{2,0},{3,1},{4,6},{5,7},{6,4},{7,5},{8,10},{9,11},{10,... | collective-permute-start | bytes 3317768 | tf_op jit(solution)/shard_map/ppermute | solution.py:238
  600.1 26.3 %collective-permute-start.37 = (bf16[1152,144]{0,1:T(8,128)(2,1)}, bf16[1152,144]{0,1:T(8,128)(2,1)}, u32[]{:S(2)}, u32[]{:S(2)}) collective-permute-start(bf16[1152,144]{0,1:T(8,128)(2,1)} %copy.35), channel_id=1, source_target_pairs={{0,4},{4,0},{8,12},{12,8},{16,20},{20,16},{24,28},{28,24},{1,5},{5... | collective-permute-start | bytes 995336 | tf_op jit(solution)/shard_map/ppermute | solution.py:238
  603.4 41.8 %collective-permute-start.35 = (bf16[288,1152]{1,0:T(8,128)(2,1)}, bf16[288,1152]{1,0:T(8,128)(2,1)}, u32[]{:S(2)}, u32[]{:S(2)}) collective-permute-start(bf16[288,1152]{1,0:T(8,128)(2,1)} %slice_select_fusion.25), channel_id=1, source_target_pairs={{0,16},{4,20},{8,24},{12,28},{16,0},{20,4},{24,8},{28,12},{1,17},{... | collective-permute-start | bytes 1990664 | tf_op jit(solution)/shard_map/ppermute | solution.py:238
  610.5 32.3 %collective-permute-start.33 = (bf16[288,288]{1,0:T(8,128)(2,1)}, bf16[288,288]{1,0:T(8,128)(2,1)}, u32[]{:S(2)}, u32[]{:S(2)}) collective-permute-start(bf16[288,288]{1,0:T(8,128)(2,1)} %broadcast_select_fusion.3), channel_id=1, source_target_pairs={{0,16},{4,20},{8,24},{12,28},{16,0},{20,4},{24,8},{28,12},{1,17},{... | collective-permute-start | bytes 497672 | tf_op jit(solution)/shard_map/ppermute | solution.py:238
  685.2 26.9 %collective-permute-start.29 = (bf16[288,1728]{1,0:T(8,128)(2,1)}, bf16[288,1728]{1,0:T(8,128)(2,1)S(1)}, u32[]{:S(2)}, u32[]{:S(2)}) collective-permute-start(bf16[288,1728]{1,0:T(8,128)(2,1)} %pad_maximum_fusion.7), channel_id=1, source_target_pairs={{0,8},{4,12},{8,0},{12,4},{16,24},{20,28},{24,16},{28,20},{1,9},{5... | collective-permute-start | bytes 2985992 | tf_op jit(solution)/shard_map/ppermute | solution.py:238
  686.4 25.5 %collective-permute-start.25 = (f32[8,1728]{1,0:T(8,128)S(1)}, f32[8,1728]{1,0:T(8,128)S(1)}, u32[]{:S(2)}, u32[]{:S(2)}) collective-permute-start(f32[8,1728]{1,0:T(8,128)S(1)} %pad_maximum_fusion.17), channel_id=1, source_target_pairs={{0,8},{4,12},{8,0},{12,4},{16,24},{20,28},{24,16},{28,20},{1,9},{5... | collective-permute-start | bytes 165896 | tf_op jit(solution)/shard_map/ppermute | solution.py:238
  696.2 19.6 %collective-permute-start.39 = (f32[16128]{0:T(1024)S(1)}, f32[16128]{0:T(1024)S(1)}, u32[]{:S(2)}, u32[]{:S(2)}) collective-permute-start(f32[16128]{0:T(1024)S(1)} %add.316), channel_id=1, source_target_pairs={{0,2},{1,3},{2,0},{3,1},{4,6},{5,7},{6,4},{7,5},{8,10},{9,11},{10,... | collective-permute-start | bytes 193544 | tf_op jit(solution)/shard_map/ppermute | solution.py:238
  712.0 17.1 %collective-permute-start.26 = (f32[16,864]{1,0:T(8,128)S(1)}, f32[16,864]{1,0:T(8,128)S(1)}, u32[]{:S(2)}, u32[]{:S(2)}) collective-permute-start(f32[16,864]{1,0:T(8,128)S(1)} %get-tuple-element.206), channel_id=1, source_target_pairs={{0,16},{4,20},{8,24},{12,28},{16,0},{20,4},{24,8},{28,12},{1,17},{... | collective-permute-start | bytes 165896 | tf_op jit(solution)/shard_map/ppermute | solution.py:238
  712.8 34.1 %collective-permute-start.30 = (bf16[288,864]{1,0:T(8,128)(2,1)S(1)}, bf16[288,864]{1,0:T(8,128)(2,1)S(1)}, u32[]{:S(2)}, u32[]{:S(2)}) collective-permute-start(bf16[288,864]{1,0:T(8,128)(2,1)S(1)} %broadcast_select_fusion), channel_id=1, source_target_pairs={{0,16},{4,20},{8,24},{12,28},{16,0},{20,4},{24,8},{28,12},{1,17},{... | collective-permute-start | bytes 1493000 | tf_op jit(solution)/shard_map/ppermute | solution.py:238
  (126 other events, 2353.6 us)
Sparse Core Ops, SparseCore 0:
  9.6 63.2 all-gather.4
  74.5 25.7 all-gather.6
  101.8 70.9 all-gather.8
  174.2 70.9 all-gather.10
